TPU v7x, 1024 devices: a whole 8x8x8 slice. The times are simulated.
1024 devices in a mesh: ctx: 128 (over y, x, core), head: 8 (over z).
Axes of the slice: x: 8, y: 8, z: 8, core: 2. Of those that a mesh axis runs over, the one named last changes fastest.
Arguments:
- queries: bfloat16 [32768, 4096], P('ctx', 'head'), may hold values from -5 to 5
- keys: bfloat16 [32768, 4096], P('ctx', 'head'), may hold values from -5 to 5
- values: bfloat16 [32768, 4096], P('ctx', 'head'), may hold values from -1300 to 1300
- gate_logits: bfloat16 [32768, 4096], P('ctx', 'head'), may hold values from -6 to 6
- norm_gain: float32 [4096], replicated, may hold values from 0.1 to 1.9
- out_weight: bfloat16 [4096, 6144], P(None, 'head'), may hold values from -0.09375 to 0.09375
- residual: bfloat16 [32768, 6144], P('ctx', 'head'), may hold values from -4 to 4
Outputs:
- layer_out: bfloat16 [32768, 6144], P('ctx', 'head')
All inputs are finite; a program needn't handle non-finite values.
Results may differ from a plain program's by a relative error of at most 0.011.
Values may be sent and summed in bfloat16 or wider, within the bound.
No kernel may reach another device: no remote copies, remote signals or barrier semaphores. Data moves between devices by JAX's collectives and lax.ppermute only.
A program may use at most 64 MiB of HBM per device.

v0:
```python
import jax
import jax.numpy as jnp
from jax import lax
from jax.sharding import PartitionSpec as P

HEAD_DIM = 128
BLOCK = 256
INNER = 4096


epsilon = 1e-06


def prefix(shard, axis, join, neutral):
    place = lax.axis_index(axis)
    gathered = lax.all_gather(shard.astype(jnp.bfloat16), axis)
    state = jnp.zeros_like(shard) + jnp.asarray(neutral, shard.dtype)

    def one(hop, state):
        return join(state, lax.dynamic_index_in_dim(gathered, hop, 0, False).astype(shard.dtype))

    return lax.fori_loop(0, place, one, state)


def add_states(earlier, later):
    return earlier + later


def on_device(queries, keys, values, gate_logits, norm_gain, out_weight, residual):
    tok_rows, feature_width = queries.shape
    heads_here = feature_width // HEAD_DIM
    block_count = tok_rows // BLOCK

    def head_columns(array, head_number):
        columns = array[:, head_number * HEAD_DIM : (head_number + 1) * HEAD_DIM]
        return columns.reshape(block_count, BLOCK, HEAD_DIM)

    state_list = []
    for head_number in range(heads_here):
        key_head = head_columns(keys, head_number)
        value_head = head_columns(values, head_number)
        state_list.append(
            jnp.einsum("bsd,bse->bde", key_head, value_head, preferred_element_type=jnp.float32)
        )
    block_state = jnp.stack(state_list, axis=1)
    own_state = jnp.sum(block_state, axis=0)
    earlier_state = prefix(own_state, "ctx", add_states, jnp.zeros_like(own_state))
    prefix_state = earlier_state[None] + (jnp.cumsum(block_state, axis=0) - block_state)
    state_high = prefix_state.astype(jnp.bfloat16)
    state_low = (prefix_state - state_high.astype(jnp.float32)).astype(jnp.bfloat16)
    causal_mask = jnp.tril(jnp.ones((BLOCK, BLOCK), dtype=bool))
    head_outputs = []
    for head_number in range(heads_here):
        query_head = head_columns(queries, head_number)
        key_head = head_columns(keys, head_number)
        value_head = head_columns(values, head_number)
        scores = jnp.einsum(
            "btd,bsd->bts", query_head, key_head, preferred_element_type=jnp.float32
        )
        scores = jnp.where(causal_mask[None], scores, jnp.float32(0.0)).astype(jnp.bfloat16)
        local_part = jnp.einsum(
            "bts,bsd->btd", scores, value_head, preferred_element_type=jnp.float32
        )
        carried_part = jnp.einsum(
            "btd,bde->bte",
            query_head,
            state_high[:, head_number],
            preferred_element_type=jnp.float32,
        )
        carried_part = carried_part + jnp.einsum(
            "btd,bde->bte",
            query_head,
            state_low[:, head_number],
            preferred_element_type=jnp.float32,
        )
        head_outputs.append((local_part + carried_part).reshape(tok_rows, HEAD_DIM))
    attended = jnp.concatenate(head_outputs, axis=1).astype(jnp.bfloat16)
    attended_float = attended.astype(jnp.float32)
    square_total = lax.psum(jnp.sum(attended_float * attended_float, axis=1), "head")
    scale_rows = lax.rsqrt(square_total / INNER + epsilon)
    gain_here = lax.dynamic_slice_in_dim(
        norm_gain, lax.axis_index("head") * feature_width, feature_width, 0
    )
    normed = (
        attended_float
        * scale_rows[:, None]
        * gain_here[None, :]
        * jax.nn.sigmoid(gate_logits.astype(jnp.float32))
    )
    normed = normed.astype(jnp.bfloat16)
    projected = jnp.dot(
        lax.all_gather(normed, "head", axis=1, tiled=True),
        out_weight,
        preferred_element_type=jnp.float32,
    )
    return (projected + residual.astype(jnp.float32)).astype(jnp.bfloat16)


def solution(mesh):
    in_specs = (
        P("ctx", "head"),
        P("ctx", "head"),
        P("ctx", "head"),
        P("ctx", "head"),
        P(),
        P(None, "head"),
        P("ctx", "head"),
    )
    out_specs = P("ctx", "head")
    return jax.shard_map(
        on_device, mesh=mesh, in_specs=in_specs, out_specs=out_specs, check_vma=False
    )
```

profile of v0, /device:TPU:2, one launch (start us, length us, event | category | flops | bytes accessed | tf_op | source)
XLA Modules:
  0.0 328.5 jit_solution(13796859439672744166)
XLA Ops:
  6.5 0.0 copy-start.3
  6.5 0.0 copy-start.2
  6.5 0.0 copy-start
  6.5 0.0 copy-start.1
  6.5 0.0 all-gather.3.cloned.1.call-start
  6.6 1.2 fusion.32
  7.7 1.1 fusion.38
  8.8 1.1 fusion.44
  9.9 1.1 fusion.49
  11.0 0.7 pad_maximum_fusion.1
  11.7 0.0 all-gather.3.cloned.1.call-update
  11.7 0.0 all-gather.5.cloned.1.call-start
  11.8 1.1 copy.9
  12.8 0.8 dynamic_slice.7
  13.6 114.5 %all-gather.3.cloned.1.call-done = bf16[128,4,128,128]{3,2,1,0:T(8,128)(2,1)} async-done(((bf16[1,4,128,128]{3,2,1,0:T(8,128)(2,1)}), bf16[128,4,128,128]{3,2,1,0:T(8,128)(2,1)}) %all-gather.3.cloned.1.call-update) | async-done | bytes 16777232 | tf_op jit(solution)/shard_map/all_gather | solution.py:16
  128.1 2.0 while.10
  128.2 1.0 convert_add_fusion.2
  129.2 1.0 convert_add_fusion.2
  130.1 0.1 fusion.26
  130.2 0.0 copy-done
  130.2 0.2 fusion.71
  130.4 0.2 fusion.66
  130.6 0.2 fusion.61
  130.8 0.2 fusion.56
  131.0 0.2 fusion.16
  131.2 0.0 copy-done.3
  131.2 0.0 copy-done.2
  131.2 0.4 fusion.17
  131.6 0.2 fusion.15
  131.8 0.4 fusion.18
  132.2 0.2 fusion.14
  132.4 0.4 fusion.19
  132.7 0.2 fusion.13
  132.9 0.4 fusion.20
  133.3 0.1 fusion.21
  133.4 19.4 %psum.7 = f32[256]{0:T(256)S(1)} all-reduce(f32[256]{0:T(256)S(1)} %fusion.21), channel_id=1, replica_groups=mesh['ctx'=128,'head'=8] {'head'}, use_global_device_ids=true, to_apply=%region_3.4 | all-reduce | flops 256 | bytes 2048 | tf_op jit(solution)/shard_map/psum | solution.py:79
  152.8 0.9 fusion.24
  153.7 0.0 all-gather.5.cloned.1.call-update
  153.7 161.9 %all-gather.5.cloned.1.call-done = bf16[256,4096]{0,1:T(8,128)(2,1)} async-done(((bf16[256,512]{0,1:T(8,128)(2,1)}), bf16[256,4096]{0,1:T(8,128)(2,1)}) %all-gather.5.cloned.1.call-update) | async-done | bytes 2097168 | tf_op jit(solution)/shard_map/all_gather | solution.py:92
  315.6 0.0 copy-done.1
  315.6 6.0 %fusion = bf16[256,768]{1,0:T(8,128)(2,1)} fusion(bf16[256,4096]{0,1:T(8,128)(2,1)} %all-gather.5.cloned.1.call-done, bf16[4096,768]{1,0:T(8,128)(2,1)} %param.14, bf16[256,768]{1,0:T(8,128)(2,1)S(1)} %copy-done.1), kind=kOutput, calls=%fused_computation.2 | convolution fusion | flops 1611202560 | bytes 9175040 | tf_op jit(solution)/shard_map/dot_general | solution.py:91
  (4 shorter events, 0.1 us)
Async XLA Ops:
  6.5 124.7 %copy-start.3 = (bf16[256,512]{1,0:T(8,128)(2,1)S(1)}, bf16[256,512]{1,0:T(8,128)(2,1)}, u32[]{:S(2)}) copy-start(bf16[256,512]{1,0:T(8,128)(2,1)} %param.10) | copy-start | bytes 786436
  6.5 124.7 %copy-start.2 = (bf16[256,512]{1,0:T(8,128)(2,1)S(1)}, bf16[256,512]{1,0:T(8,128)(2,1)}, u32[]{:S(2)}) copy-start(bf16[256,512]{1,0:T(8,128)(2,1)} %param.11) | copy-start | bytes 786436
  6.5 123.7 %copy-start = (bf16[256,512]{1,0:T(8,128)(2,1)S(1)}, bf16[256,512]{1,0:T(8,128)(2,1)}, u32[]{:S(2)}) copy-start(bf16[256,512]{1,0:T(8,128)(2,1)} %param.9) | copy-start | bytes 786436
  6.5 309.1 %copy-start.1 = (bf16[256,768]{1,0:T(8,128)(2,1)S(1)}, bf16[256,768]{1,0:T(8,128)(2,1)}, u32[]{:S(2)}) copy-start(bf16[256,768]{1,0:T(8,128)(2,1)} %param.15) | copy-start | bytes 1179652
  6.5 121.6 %all-gather.3.cloned.1.call-start = ((), (), s32[]{:S(2)}) async-start(), calls=%async_computation | async-start | bytes 16908288 | tf_op jit(solution)/shard_map/all_gather | solution.py:16
  11.7 303.9 %all-gather.5.cloned.1.call-start = ((), (), s32[]{:S(2)}) async-start(), calls=%async_computation.1 | async-start | bytes 2359296 | tf_op jit(solution)/shard_map/all_gather | solution.py:92
Sparse Core Ops, SparseCore 0:
  11.8 116.2 all-gather.2
  153.8 161.7 all-gather.4
where the time goes:
time: 331 us; the launch traced here: 328 us
  waiting for transfers between devices  276 us (83%)
  blocking collectives  19.4 us (6%)
  between operations  13.5 us (4%)
  matrix products  13.4 us (4%)
  other arithmetic  3.68 us (1%)
    all_gather x1, waiting for transfers between devices, on_device(): lax.all_gather(normed, 'head', axis=1, tiled=True)  162 us
    all_gather x1, waiting for transfers between devices, prefix(): gathered = lax.all_gather(shard.astype(jnp.bfloat16), axis)  115 us
    psum x1, blocking collectives, on_device(): lax.psum(jnp.sum(attended_float * attended_float, axis=1), 'head')  19.4 us
  transfers between devices with their start and end apart: 2, of which 2 were waited for; matrix products, arithmetic and copies ran while one was open for 1% of the time, Pallas kernels for 0%

commit v1 on v0

v1 whole, which is shorter than its diff:
```python
import jax
import jax.numpy as jnp
from jax import lax
from jax.experimental import pallas as pl
from jax.experimental.pallas import tpu as pltpu
from jax.sharding import Mesh, PartitionSpec as P

HEAD_DIM = 128
BLOCK = 256
INNER = 4096
SIDE = 8
CORES = 2

epsilon = 1e-06
f32 = jnp.float32
bf16 = jnp.bfloat16


def call(kernel, out_shape, *args, flops=0, smem=0):
    size = sum(a.size * a.dtype.itemsize for a in args)
    return pl.pallas_call(
        kernel,
        out_shape=out_shape,
        in_specs=[pl.BlockSpec(memory_space=pltpu.SMEM)] * smem
        + [pl.BlockSpec(memory_space=pltpu.VMEM)] * (len(args) - smem),
        out_specs=jax.tree.map(lambda _: pl.BlockSpec(memory_space=pltpu.VMEM), out_shape),
        cost_estimate=pl.CostEstimate(flops=flops, bytes_accessed=size, transcendentals=0),
    )(*args)


def heads_of(ref):
    return [slice(h * HEAD_DIM, (h + 1) * HEAD_DIM) for h in range(ref.shape[1] // HEAD_DIM)]


def state_kernel(keys, values, out):
    rows = out.shape[1]
    per = HEAD_DIM // rows
    for h, cols in enumerate(heads_of(keys)):
        state = lax.dot_general(
            keys[:, cols], values[:, cols], (((0,), (0,)), ((), ())), preferred_element_type=f32
        )
        out[h * per : (h + 1) * per] = state.reshape(per, rows, HEAD_DIM).astype(bf16)


def total_kernel(row, out):
    total = row[0].astype(f32)
    for member in range(1, row.shape[0]):
        total = total + row[member].astype(f32)
    out[...] = jnp.broadcast_to(total.astype(bf16)[None], out.shape)


def prefix_kernel(place, row, totals, out):
    mine = place[0]
    run = jnp.zeros(row.shape[1:], f32)
    for other in range(totals.shape[0]):
        run = run + jnp.where(other < mine, totals[other].astype(f32), 0.0)
    for member in range(row.shape[0]):
        out[member] = run.astype(bf16)
        run = run + row[member].astype(f32)


def local_kernel(queries, keys, values, gates, gain, local, gated):
    tokens = queries.shape[0]
    later = lax.broadcasted_iota(jnp.int32, (tokens, tokens), 0)
    earlier = lax.broadcasted_iota(jnp.int32, (tokens, tokens), 1)
    for cols in heads_of(queries):
        scores = lax.dot_general(
            queries[:, cols], keys[:, cols], (((1,), (1,)), ((), ())), preferred_element_type=f32
        )
        scores = jnp.where(earlier <= later, scores, 0.0).astype(bf16)
        local[:, cols] = jnp.dot(scores, values[:, cols], preferred_element_type=f32)
    gated[...] = gain[...] * jax.nn.sigmoid(gates[...].astype(f32))


def attend_kernel(queries, state, local, gated, out):
    tokens = queries.shape[0]
    squares = jnp.zeros((tokens, 1), f32)
    for h, cols in enumerate(heads_of(queries)):
        part = jnp.dot(queries[:, cols], state[h], preferred_element_type=f32)
        attended = (local[:, cols] + part).astype(bf16).astype(f32)
        squares = squares + jnp.sum(attended * attended, axis=1, keepdims=True)
        out[:tokens, cols] = (attended * gated[:, cols]).astype(bf16)
    lane = lax.broadcasted_iota(jnp.int32, (tokens, HEAD_DIM), 1)
    high = squares.astype(bf16).astype(f32)
    middle = (squares - high).astype(bf16).astype(f32)
    low = squares - high - middle
    packed = jnp.where(lane == 0, high, jnp.where(lane == 1, middle, jnp.where(lane == 2, low, 0.0)))
    extra = out.shape[0] - tokens
    out[tokens:, :tokens] = packed.T[:extra].astype(bf16)
    out[tokens:, tokens:] = jnp.zeros((extra, out.shape[1] - tokens), bf16)


def exchange(blocks, axes):
    return lax.all_to_all(blocks, axes, 0, 0, tiled=True)


def shift(block, hops):
    pairs = [(place, (place + hops) % SIDE) for place in range(SIDE)]
    return lax.ppermute(block, "z", pairs)


def on_device(queries, keys, values, gate_logits, norm_gain, out_weight, residual):
    tokens, width = queries.shape
    heads = width // HEAD_DIM
    row_places = SIDE * CORES
    rows = heads * HEAD_DIM // row_places
    z = lax.axis_index("z")
    shape = jax.ShapeDtypeStruct

    own = call(
        state_kernel, shape((row_places, rows, HEAD_DIM), bf16), keys, values,
        flops=2 * tokens * width * HEAD_DIM,
    )
    row = exchange(own, ("x", "core"))
    totals = call(total_kernel, shape((SIDE, rows, HEAD_DIM), bf16), row)
    totals = exchange(totals, "y")
    place = lax.axis_index("y").reshape(1)
    state = call(
        prefix_kernel, shape((row_places, rows, HEAD_DIM), bf16), place, row, totals, smem=1
    )
    state = exchange(state, ("x", "core")).reshape(heads, HEAD_DIM, HEAD_DIM)

    gain_here = lax.dynamic_slice_in_dim(norm_gain, z * width, width, 0)[None]
    local, gated = call(
        local_kernel, [shape((tokens, width), f32)] * 2,
        queries, keys, values, gate_logits, gain_here,
        flops=4 * tokens * tokens * width,
    )
    block = call(
        attend_kernel, shape((tokens + 16, width), bf16), queries, state, local, gated,
        flops=2 * tokens * width * HEAD_DIM,
    )

    def product(piece, offset):
        source = lax.rem(z + offset + SIDE, SIDE)
        weight = lax.dynamic_slice_in_dim(out_weight, source * width, width, 0)
        return jnp.dot(piece[:tokens], weight, preferred_element_type=f32)

    def squares(piece):
        return jnp.sum(piece[tokens : tokens + 3, :tokens].astype(f32), axis=0)

    half = tokens // 2
    up1, down1 = shift(block, -1), shift(block, 1)
    up2, down2 = shift(up1, -1), shift(down1, 1)
    up3, down3 = shift(up2, -1), shift(down2, 1)
    far = jnp.concatenate([shift(up2[:half], -2), shift(down2[half:], 2)], axis=0)
    pieces = [(block, 0), (up1, 1), (down1, -1), (up2, 2), (down2, -2), (up3, 3), (down3, -3), (far, 4)]
    total = jnp.zeros((tokens,), f32)
    projected = None
    for piece, offset in pieces:
        total = total + squares(piece)
        part = product(piece, offset)
        projected = part if projected is None else projected + part
    scale_rows = lax.rsqrt(total / INNER + epsilon)
    return (projected * scale_rows[:, None] + residual.astype(f32)).astype(bf16)


def solution(mesh):
    split = Mesh(mesh.devices.reshape(SIDE, SIDE, CORES, SIDE), ("y", "x", "core", "z"))
    ctx = ("y", "x", "core")
    in_specs = (
        P(ctx, "z"),
        P(ctx, "z"),
        P(ctx, "z"),
        P(ctx, "z"),
        P(),
        P(None, "z"),
        P(ctx, "z"),
    )
    return jax.shard_map(
        on_device, mesh=split, in_specs=in_specs, out_specs=P(ctx, "z"), check_vma=False
    )
```

time: 331 us -> 111 us (0.34)
  the two profiles are of different devices: /device:TPU:2 before, /device:TPU:1 now
where the time goes in v1:
time: 111 us; the launch traced here: 110 us
  starting transfers between devices  41.2 us (37%)
  blocking collectives  27.3 us (25%)
  waiting for transfers between devices  19.9 us (18%)
  Pallas kernels  10.6 us (10%)
  matrix products  7.33 us (7%)
  local copies, waits for them, and re-layouts  2.64 us (2%)
    ppermute x8, starting transfers between devices, shift(): return lax.ppermute(block, 'z', pairs)  33.7 us
    all_to_all x1, blocking collectives, exchange(): return lax.all_to_all(blocks, axes, 0, 0, tiled=True)  27.3 us
    all_to_all x2, waiting for transfers between devices, exchange(): return lax.all_to_all(blocks, axes, 0, 0, tiled=True)  12.8 us
    pallas_call x5, Pallas kernels, call(): pl.pallas_call(kernel, out_shape=out_shape, in_specs=[pl.BlockSpec(memory...  10.6 us
    all_to_all x2, starting transfers between devices, exchange(): return lax.all_to_all(blocks, axes, 0, 0, tiled=True)  7.43 us
    dot_general x8, matrix products, product(): return jnp.dot(piece[:tokens], weight, preferred_element_type=f32)  7.33 us
    ppermute x8, waiting for transfers between devices, shift(): return lax.ppermute(block, 'z', pairs)  7.15 us
  transfers between devices with their start and end apart: 10, of which 6 were waited for; matrix products, arithmetic and copies ran while one was open for 7% of the time, Pallas kernels for 3%

profile of v1, /device:TPU:1, one launch (start us, length us, event | category | flops | bytes accessed | tf_op | source)
XLA Modules:
  0.0 110.0 jit_solution(5611366051611290024)
XLA Ops:
  0.0 0.0 slice-start
  0.0 2.1 %shard_map.73 = bf16[16,32,128]{2,1,0:T(8,128)(2,1)} custom-call(bf16[256,512]{1,0:T(8,128)(2,1)} %keys.3, bf16[256,512]{1,0:T(8,128)(2,1)} %values.3), custom_call_target="tpu_custom_call" | custom-call | flops 33554432 | bytes 524288 | tf_op jit(solution)/shard_map/pallas_call | solution.py:21
  2.1 27.3 %all_to_all.15.row = bf16[16,32,128]{2,1,0:T(8,128)(2,1)} all-to-all(bf16[16,32,128]{2,1,0:T(8,128)(2,1)} %shard_map.73), channel_id=1, replica_groups=mesh['y'=8,'x'=8,'core'=2,'z'=8] {'x','core'}, dimensions={0} | all-to-all | bytes 262144 | tf_op jit(solution)/shard_map/all_to_all | solution.py:94
  29.4 1.6 %shard_map.74 = bf16[8,32,128]{2,1,0:T(8,128)(2,1)} custom-call(bf16[16,32,128]{2,1,0:T(8,128)(2,1)} %all_to_all.15.row), custom_call_target="tpu_custom_call" | custom-call | bytes 131072 | tf_op jit(solution)/shard_map/pallas_call | solution.py:21
  30.9 3.4 %all-to-all-start.1 = ((bf16[8,32,128]{2,1,0:T(8,128)(2,1)}), bf16[8,32,128]{2,1,0:T(8,128)(2,1)S(1)}, u32[]{:S(2)}, u32[]{:S(2)}) async-start(bf16[8,32,128]{2,1,0:T(8,128)(2,1)} %shard_map.74), calls=%async_computation.1 | async-start | bytes 131072 | tf_op jit(solution)/shard_map/all_to_all | solution.py:94
  34.3 7.7 %all-to-all-done.1.totals = bf16[8,32,128]{2,1,0:T(8,128)(2,1)S(1)} async-done(((bf16[8,32,128]{2,1,0:T(8,128)(2,1)}), bf16[8,32,128]{2,1,0:T(8,128)(2,1)S(1)}, u32[]{:S(2)}, u32[]{:S(2)}) %all-to-all-start.1) | async-done | bytes 65568 | tf_op jit(solution)/shard_map/all_to_all | solution.py:94
  42.1 0.0 copy-start.2
  42.1 0.6 copy-done.2
  42.7 1.6 %shard_map.75 = bf16[16,32,128]{2,1,0:T(8,128)(2,1)} custom-call(s32[1]{0:T(128)} %bitcast.place, bf16[16,32,128]{2,1,0:T(8,128)(2,1)} %all_to_all.15.row, bf16[8,32,128]{2,1,0:T(8,128)(2,1)} %copy-done.2), custom_call_target="tpu_custom_call" | custom-call | bytes 196612 | tf_op jit(solution)/shard_map/pallas_call | solution.py:21
  44.3 4.1 %all-to-all-start.2 = ((bf16[16,32,128]{2,1,0:T(8,128)(2,1)}), bf16[16,32,128]{2,1,0:T(8,128)(2,1)S(1)}, u32[]{:S(2)}, u32[]{:S(2)}) async-start(bf16[16,32,128]{2,1,0:T(8,128)(2,1)} %shard_map.75), calls=%async_computation.2 | async-start | bytes 262144 | tf_op jit(solution)/shard_map/all_to_all | solution.py:94
  48.4 1.3 %dynamic_slice.27 = f32[512]{0:T(512)} dynamic-slice(f32[4096]{0:T(1024)} %param.11, s32[]{:T(128)S(6)} %select_n.27), dynamic_slice_sizes={512} | dynamic-slice | bytes 4100 | tf_op jit(solution)/shard_map/dynamic_slice | solution.py:123
  49.7 2.8 %shard_map.76 = (f32[256,512]{1,0:T(8,128)}, f32[256,512]{1,0:T(8,128)}) custom-call(bf16[256,512]{1,0:T(8,128)(2,1)} %queries.3, bf16[256,512]{1,0:T(8,128)(2,1)} %keys.3, bf16[256,512]{1,0:T(8,128)(2,1)} %values.3, bf16[256,512]{1,0:T(8,128)(2,1)} %gates.1, f32[1,512]{1,0:T(1,128)} %bitcast.6), custom_call_target="tpu_custom_call" | custom-call | flops 134217728 | bytes 1050624 | tf_op jit(solution)/shard_map/pallas_call | solution.py:21
  52.5 5.0 %all-to-all-done.2 = bf16[16,32,128]{2,1,0:T(8,128)(2,1)S(1)} async-done(((bf16[16,32,128]{2,1,0:T(8,128)(2,1)}), bf16[16,32,128]{2,1,0:T(8,128)(2,1)S(1)}, u32[]{:S(2)}, u32[]{:S(2)}) %all-to-all-start.2) | async-done | bytes 131104 | tf_op jit(solution)/shard_map/all_to_all | solution.py:94
  57.5 0.0 copy-start
  57.5 0.6 copy-done
  58.2 2.5 %shard_map.77 = bf16[272,512]{1,0:T(8,128)(2,1)} custom-call(bf16[256,512]{1,0:T(8,128)(2,1)} %queries.3, bf16[4,128,128]{2,1,0:T(8,128)(2,1)} %bitcast.5, f32[256,512]{1,0:T(8,128)} %get-tuple-element.7.local, f32[256,512]{1,0:T(8,128)} %get-tuple-element.8.gated), custom_call_target="tpu_custom_call" | custom-call | flops 33554432 | bytes 1441792 | tf_op jit(solution)/shard_map/pallas_call | solution.py:21
  60.7 0.0 slice-start.1
  60.7 2.2 %collective-permute-start.1 = (bf16[272,512]{1,0:T(8,128)(2,1)}, bf16[272,512]{1,0:T(8,128)(2,1)S(1)}, u32[]{:S(2)}, u32[]{:S(2)}) collective-permute-start(bf16[272,512]{1,0:T(8,128)(2,1)} %shard_map.77), channel_id=1, source_target_pairs={{0,1},{1,2},{2,3},{3,4},{4,5},{5,6},{6,7},{7,0},{8,9},{9,10},{10,1... | collective-permute-start | bytes 835592 | tf_op jit(solution)/shard_map/ppermute | solution.py:99
  62.8 11.0 %collective-permute-start = (bf16[272,512]{1,0:T(8,128)(2,1)}, bf16[272,512]{1,0:T(8,128)(2,1)S(1)}, u32[]{:S(2)}, u32[]{:S(2)}) collective-permute-start(bf16[272,512]{1,0:T(8,128)(2,1)} %shard_map.77), channel_id=1, source_target_pairs={{0,7},{1,0},{2,1},{3,2},{4,3},{5,4},{6,5},{7,6},{8,15},{9,8},{10,9... | collective-permute-start | bytes 835592 | tf_op jit(solution)/shard_map/ppermute | solution.py:99
  73.9 1.6 %fusion.16 = f32[256,768]{1,0:T(8,128)S(1)} fusion(bf16[4096,768]{1,0:T(8,128)(2,1)} %param.12, s32[]{:T(128)S(6)} %select_n.28, bf16[272,512]{1,0:T(8,128)(2,1)} %shard_map.77), kind=kOutput, calls=%fused_computation.20 | convolution fusion | flops 201326592 | bytes 1835012 | tf_op jit(solution)/shard_map/dot_general | solution.py:137
  75.5 0.7 convert_reduce_fusion.7
  76.2 2.8 %collective-permute-done.1 = bf16[272,512]{1,0:T(8,128)(2,1)S(1)} collective-permute-done((bf16[272,512]{1,0:T(8,128)(2,1)}, bf16[272,512]{1,0:T(8,128)(2,1)S(1)}, u32[]{:S(2)}, u32[]{:S(2)}) %collective-permute-start.1) | collective-permute-done | bytes 278560 | tf_op jit(solution)/shard_map/ppermute | solution.py:99
  79.0 1.9 %collective-permute-start.3 = (bf16[272,512]{1,0:T(8,128)(2,1)S(1)}, bf16[272,512]{1,0:T(8,128)(2,1)S(1)}, u32[]{:S(2)}, u32[]{:S(2)}) collective-permute-start(bf16[272,512]{1,0:T(8,128)(2,1)S(1)} %collective-permute-done.1), channel_id=1, source_target_pairs={{0,1},{1,2},{2,3},{3,4},{4,5},{5,6},{6,7},{7,0},{8,9},{9,10},{10,1... | collective-permute-start | bytes 835592 | tf_op jit(solution)/shard_map/ppermute | solution.py:99
  80.9 0.0 collective-permute-done
  81.0 4.8 %collective-permute-start.2 = (bf16[272,512]{1,0:T(8,128)(2,1)S(1)}, bf16[272,512]{1,0:T(8,128)(2,1)S(1)}, u32[]{:S(2)}, u32[]{:S(2)}) collective-permute-start(bf16[272,512]{1,0:T(8,128)(2,1)S(1)} %collective-permute-done), channel_id=1, source_target_pairs={{0,7},{1,0},{2,1},{3,2},{4,3},{5,4},{6,5},{7,6},{8,15},{9,8},{10,9... | collective-permute-start | bytes 835592 | tf_op jit(solution)/shard_map/ppermute | solution.py:99
  85.7 1.5 %convolution_add_fusion.3 = f32[256,768]{1,0:T(8,128)S(1)} fusion(f32[256,768]{1,0:T(8,128)S(1)} %fusion.16, bf16[4096,768]{1,0:T(8,128)(2,1)} %param.12, s32[]{:T(128)S(6)} %select_n.29, bf16[272,512]{1,0:T(8,128)(2,1)S(1)} %collective-permute-done), kind=kOutput, calls=%fused_computation.8 | convolution fusion | flops 201523200 | bytes 2621444 | tf_op jit(solution)/shard_map/dot_general | solution.py:137
  87.2 0.0 copy-start.1
  87.3 1.5 %convolution_add_fusion.2 = f32[256,768]{1,0:T(8,128)S(1)} fusion(f32[256,768]{1,0:T(8,128)S(1)} %convolution_add_fusion.3, bf16[4096,768]{1,0:T(8,128)(2,1)} %param.12, s32[]{:T(128)S(6)} %select_n.30, bf16[272,512]{1,0:T(8,128)(2,1)S(1)} %collective-permute-done.1), kind=kOutput, calls=%fused_computation.7 | convolution fusion | flops 201523200 | bytes 2621444 | tf_op jit(solution)/shard_map/dot_general | solution.py:137
  88.8 1.1 collective-permute-done.3
  89.9 1.9 %collective-permute-start.7 = (bf16[144,512]{1,0:T(8,128)(2,1)S(1)}, bf16[144,512]{1,0:T(8,128)(2,1)S(1)}, u32[]{:S(2)}, u32[]{:S(2)}) collective-permute-start(bf16[144,512]{1,0:T(8,128)(2,1)S(1)} %slice.80), channel_id=1, source_target_pairs={{0,2},{1,3},{2,4},{3,5},{4,6},{5,7},{6,0},{7,1},{8,10},{9,11},{10,... | collective-permute-start | bytes 442376 | tf_op jit(solution)/shard_map/ppermute | solution.py:99
  91.9 0.0 collective-permute-done.2
  91.9 5.5 %collective-permute-start.6 = (bf16[128,512]{1,0:T(8,128)(2,1)S(1)}, bf16[128,512]{1,0:T(8,128)(2,1)S(1)}, u32[]{:S(2)}, u32[]{:S(2)}) collective-permute-start(bf16[128,512]{1,0:T(8,128)(2,1)S(1)} %slice.79), channel_id=1, source_target_pairs={{0,6},{1,7},{2,0},{3,1},{4,2},{5,3},{6,4},{7,5},{8,14},{9,15},{10,... | collective-permute-start | bytes 393224 | tf_op jit(solution)/shard_map/ppermute | solution.py:99
  97.4 2.3 %collective-permute-start.5 = (bf16[272,512]{1,0:T(8,128)(2,1)S(1)}, bf16[272,512]{1,0:T(8,128)(2,1)S(1)}, u32[]{:S(2)}, u32[]{:S(2)}) collective-permute-start(bf16[272,512]{1,0:T(8,128)(2,1)S(1)} %collective-permute-done.3), channel_id=1, source_target_pairs={{0,1},{1,2},{2,3},{3,4},{4,5},{5,6},{6,7},{7,0},{8,9},{9,10},{10,1... | collective-permute-start | bytes 835592 | tf_op jit(solution)/shard_map/ppermute | solution.py:99
  99.7 4.2 %collective-permute-start.4 = (bf16[272,512]{1,0:T(8,128)(2,1)S(1)}, bf16[272,512]{1,0:T(8,128)(2,1)S(1)}, u32[]{:S(2)}, u32[]{:S(2)}) collective-permute-start(bf16[272,512]{1,0:T(8,128)(2,1)S(1)} %collective-permute-done.2), channel_id=1, source_target_pairs={{0,7},{1,0},{2,1},{3,2},{4,3},{5,4},{6,5},{7,6},{8,15},{9,8},{10,9... | collective-permute-start | bytes 835592 | tf_op jit(solution)/shard_map/ppermute | solution.py:99
  103.9 0.0 slice-done
  103.9 0.0 slice-done.1
  103.9 0.4 fusion.11
  104.3 0.4 fusion.4
  104.7 0.0 collective-permute-done.7
  104.7 0.0 collective-permute-done.6
  104.8 0.4 fusion.6
  105.1 1.7 %collective-permute-done.5 = bf16[272,512]{1,0:T(8,128)(2,1)S(1)} collective-permute-done((bf16[272,512]{1,0:T(8,128)(2,1)S(1)}, bf16[272,512]{1,0:T(8,128)(2,1)S(1)}, u32[]{:S(2)}, u32[]{:S(2)}) %collective-permute-start.5) | collective-permute-done | bytes 278560 | tf_op jit(solution)/shard_map/ppermute | solution.py:99
  106.9 1.5 %collective-permute-done.4 = bf16[272,512]{1,0:T(8,128)(2,1)S(1)} collective-permute-done((bf16[272,512]{1,0:T(8,128)(2,1)S(1)}, bf16[272,512]{1,0:T(8,128)(2,1)S(1)}, u32[]{:S(2)}, u32[]{:S(2)}) %collective-permute-start.4) | collective-permute-done | bytes 278560 | tf_op jit(solution)/shard_map/ppermute | solution.py:99
  108.4 0.4 fusion.8
  108.8 0.0 copy-done.1
  108.8 1.2 %fusion.5 = bf16[256,768]{1,0:T(8,128)(2,1)} fusion(f32[256,768]{1,0:T(8,128)S(1)} %fusion.6, f32[256,768]{1,0:T(8,128)S(1)} %fusion.8, f32[256,768]{1,0:T(8,128)S(1)} %fusion.4, bf16[256,768]{1,0:T(8,128)(2,1)S(1)} %copy-done.1, bf16[4096,768]{1,0:T(8,128)(2,1)S(1)} %bitcast.4, s32[]{:T(128)S(6)} %select_n.33, f32[256]{0:T(256)S(1)} %add_rsqrt_fusion, ...), kind=kOutput, calls=%fused_computation.9 | convolution fusion | flops 202702848 | bytes 4195332 | tf_op jit(solution)/shard_map/dot_general | solution.py:137
  (11 shorter events, 0.2 us)
Async XLA Ops:
  0.0 103.9 %slice-start = ((s8[6291456]{0:T(1024)(128)(4,1)}), s8[2097152]{0:T(1024)(128)(4,1)S(1)}, s32[]{:S(2)}) async-start(s8[6291456]{0:T(1024)(128)(4,1)} %bitcast.3), calls=%async_computation.3 | async-start | bytes 4194304
  30.9 11.1 %all-to-all-start.1 = ((bf16[8,32,128]{2,1,0:T(8,128)(2,1)}), bf16[8,32,128]{2,1,0:T(8,128)(2,1)S(1)}, u32[]{:S(2)}, u32[]{:S(2)}) async-start(bf16[8,32,128]{2,1,0:T(8,128)(2,1)} %shard_map.74), calls=%async_computation.1 | async-start | bytes 131072 | tf_op jit(solution)/shard_map/all_to_all | solution.py:94
  42.1 0.6 copy-start.2
  44.3 13.3 %all-to-all-start.2 = ((bf16[16,32,128]{2,1,0:T(8,128)(2,1)}), bf16[16,32,128]{2,1,0:T(8,128)(2,1)S(1)}, u32[]{:S(2)}, u32[]{:S(2)}) async-start(bf16[16,32,128]{2,1,0:T(8,128)(2,1)} %shard_map.75), calls=%async_computation.2 | async-start | bytes 262144 | tf_op jit(solution)/shard_map/all_to_all | solution.py:94
  57.5 0.6 copy-start
  60.7 43.2 %slice-start.1 = ((s8[6291456]{0:T(1024)(128)(4,1)}), s8[4194304]{0:T(1024)(128)(4,1)S(1)}, s32[]{:S(2)}) async-start(s8[6291456]{0:T(1024)(128)(4,1)} %bitcast.3), calls=%async_computation.4 | async-start | bytes 8388608
  60.7 18.3 %collective-permute-start.1 = (bf16[272,512]{1,0:T(8,128)(2,1)}, bf16[272,512]{1,0:T(8,128)(2,1)S(1)}, u32[]{:S(2)}, u32[]{:S(2)}) collective-permute-start(bf16[272,512]{1,0:T(8,128)(2,1)} %shard_map.77), channel_id=1, source_target_pairs={{0,1},{1,2},{2,3},{3,4},{4,5},{5,6},{6,7},{7,0},{8,9},{9,10},{10,1... | collective-permute-start | bytes 835592 | tf_op jit(solution)/shard_map/ppermute | solution.py:99
  62.8 18.1 %collective-permute-start = (bf16[272,512]{1,0:T(8,128)(2,1)}, bf16[272,512]{1,0:T(8,128)(2,1)S(1)}, u32[]{:S(2)}, u32[]{:S(2)}) collective-permute-start(bf16[272,512]{1,0:T(8,128)(2,1)} %shard_map.77), channel_id=1, source_target_pairs={{0,7},{1,0},{2,1},{3,2},{4,3},{5,4},{6,5},{7,6},{8,15},{9,8},{10,9... | collective-permute-start | bytes 835592 | tf_op jit(solution)/shard_map/ppermute | solution.py:99
  79.0 10.9 %collective-permute-start.3 = (bf16[272,512]{1,0:T(8,128)(2,1)S(1)}, bf16[272,512]{1,0:T(8,128)(2,1)S(1)}, u32[]{:S(2)}, u32[]{:S(2)}) collective-permute-start(bf16[272,512]{1,0:T(8,128)(2,1)S(1)} %collective-permute-done.1), channel_id=1, source_target_pairs={{0,1},{1,2},{2,3},{3,4},{4,5},{5,6},{6,7},{7,0},{8,9},{9,10},{10,1... | collective-permute-start | bytes 835592 | tf_op jit(solution)/shard_map/ppermute | solution.py:99
  81.0 10.9 %collective-permute-start.2 = (bf16[272,512]{1,0:T(8,128)(2,1)S(1)}, bf16[272,512]{1,0:T(8,128)(2,1)S(1)}, u32[]{:S(2)}, u32[]{:S(2)}) collective-permute-start(bf16[272,512]{1,0:T(8,128)(2,1)S(1)} %collective-permute-done), channel_id=1, source_target_pairs={{0,7},{1,0},{2,1},{3,2},{4,3},{5,4},{6,5},{7,6},{8,15},{9,8},{10,9... | collective-permute-start | bytes 835592 | tf_op jit(solution)/shard_map/ppermute | solution.py:99
  87.2 21.5 %copy-start.1 = (bf16[256,768]{1,0:T(8,128)(2,1)S(1)}, bf16[256,768]{1,0:T(8,128)(2,1)}, u32[]{:S(2)}) copy-start(bf16[256,768]{1,0:T(8,128)(2,1)} %param.13) | copy-start | bytes 1179652
  89.9 14.8 %collective-permute-start.7 = (bf16[144,512]{1,0:T(8,128)(2,1)S(1)}, bf16[144,512]{1,0:T(8,128)(2,1)S(1)}, u32[]{:S(2)}, u32[]{:S(2)}) collective-permute-start(bf16[144,512]{1,0:T(8,128)(2,1)S(1)} %slice.80), channel_id=1, source_target_pairs={{0,2},{1,3},{2,4},{3,5},{4,6},{5,7},{6,0},{7,1},{8,10},{9,11},{10,... | collective-permute-start | bytes 442376 | tf_op jit(solution)/shard_map/ppermute | solution.py:99
  91.9 12.9 %collective-permute-start.6 = (bf16[128,512]{1,0:T(8,128)(2,1)S(1)}, bf16[128,512]{1,0:T(8,128)(2,1)S(1)}, u32[]{:S(2)}, u32[]{:S(2)}) collective-permute-start(bf16[128,512]{1,0:T(8,128)(2,1)S(1)} %slice.79), channel_id=1, source_target_pairs={{0,6},{1,7},{2,0},{3,1},{4,2},{5,3},{6,4},{7,5},{8,14},{9,15},{10,... | collective-permute-start | bytes 393224 | tf_op jit(solution)/shard_map/ppermute | solution.py:99
  97.4 9.5 %collective-permute-start.5 = (bf16[272,512]{1,0:T(8,128)(2,1)S(1)}, bf16[272,512]{1,0:T(8,128)(2,1)S(1)}, u32[]{:S(2)}, u32[]{:S(2)}) collective-permute-start(bf16[272,512]{1,0:T(8,128)(2,1)S(1)} %collective-permute-done.3), channel_id=1, source_target_pairs={{0,1},{1,2},{2,3},{3,4},{4,5},{5,6},{6,7},{7,0},{8,9},{9,10},{10,1... | collective-permute-start | bytes 835592 | tf_op jit(solution)/shard_map/ppermute | solution.py:99
  99.7 8.7 %collective-permute-start.4 = (bf16[272,512]{1,0:T(8,128)(2,1)S(1)}, bf16[272,512]{1,0:T(8,128)(2,1)S(1)}, u32[]{:S(2)}, u32[]{:S(2)}) collective-permute-start(bf16[272,512]{1,0:T(8,128)(2,1)S(1)} %collective-permute-done.2), channel_id=1, source_target_pairs={{0,7},{1,0},{2,1},{3,2},{4,3},{5,4},{6,5},{7,6},{8,15},{9,8},{10,9... | collective-permute-start | bytes 835592 | tf_op jit(solution)/shard_map/ppermute | solution.py:99

commit v2 on v1

--- a/solution.py
+++ b/solution.py
@@ -10,6 +10,7 @@
 INNER = 4096
 SIDE = 8
 CORES = 2
+LIMIT = 12 * 2**20
 
 epsilon = 1e-06
 f32 = jnp.float32
@@ -24,6 +25,7 @@
         in_specs=[pl.BlockSpec(memory_space=pltpu.SMEM)] * smem
         + [pl.BlockSpec(memory_space=pltpu.VMEM)] * (len(args) - smem),
         out_specs=jax.tree.map(lambda _: pl.BlockSpec(memory_space=pltpu.VMEM), out_shape),
+        compiler_params=pltpu.CompilerParams(vmem_limit_bytes=LIMIT),
         cost_estimate=pl.CostEstimate(flops=flops, bytes_accessed=size, transcendentals=0),
     )(*args)
 
@@ -94,9 +96,14 @@
     return lax.all_to_all(blocks, axes, 0, 0, tiled=True)
 
 
-def shift(block, hops):
-    pairs = [(place, (place + hops) % SIDE) for place in range(SIDE)]
-    return lax.ppermute(block, "z", pairs)
+def hop(block):
+    upward = [(z, (z + 1) % SIDE) for z in range(SIDE)]
+    downward = [(SIDE + z, SIDE + (z - 1) % SIDE) for z in range(SIDE)]
+    return lax.ppermute(block, ("core", "z"), upward + downward)
+
+
+def swap(block):
+    return lax.ppermute(block, "core", [(0, 1), (1, 0)])
 
 
 def on_device(queries, keys, values, gate_logits, norm_gain, out_weight, residual):
@@ -131,20 +138,22 @@
         flops=2 * tokens * width * HEAD_DIM,
     )
 
+    behind = 2 * lax.axis_index("core") - 1
+
     def product(piece, offset):
-        source = lax.rem(z + offset + SIDE, SIDE)
+        source = lax.rem(z + offset * behind + SIDE, SIDE)
         weight = lax.dynamic_slice_in_dim(out_weight, source * width, width, 0)
         return jnp.dot(piece[:tokens], weight, preferred_element_type=f32)
 
     def squares(piece):
         return jnp.sum(piece[tokens : tokens + 3, :tokens].astype(f32), axis=0)
 
-    half = tokens // 2
-    up1, down1 = shift(block, -1), shift(block, 1)
-    up2, down2 = shift(up1, -1), shift(down1, 1)
-    up3, down3 = shift(up2, -1), shift(down2, 1)
-    far = jnp.concatenate([shift(up2[:half], -2), shift(down2[half:], 2)], axis=0)
-    pieces = [(block, 0), (up1, 1), (down1, -1), (up2, 2), (down2, -2), (up3, 3), (down3, -3), (far, 4)]
+    mine, other = block, swap(block)
+    pieces = [(block, 0)]
+    for step in range(1, SIDE // 2):
+        mine, other = hop(mine), hop(other)
+        pieces += [(mine, step), (swap(other), -step)]
+    pieces.append((hop(mine), SIDE // 2))
     total = jnp.zeros((tokens,), f32)
     projected = None
     for piece, offset in pieces:

time: 111 us -> 110 us (level)
  Pallas kernels: 10.6 us -> 2.7 us
  starting transfers between devices: 41.2 us -> 48.5 us
  local copies, waits for them, and re-layouts: 2.64 us -> 7.42 us
  waiting for transfers between devices: 19.9 us -> 16.5 us
  blocking collectives: 27.3 us -> 25.7 us
    pallas_call x5, Pallas kernels: 10.6 us -> 2.7 us  [call(): pl.pallas_call(kernel, out_shape=out_shape, in_specs=[pl.BlockSpec(memory...]
    ppermute x8 -> x11, starting transfers between devices: 33.7 us -> 41.1 us  [the longest x7 33.4 us: hop(): return lax.ppermute(block, ('core', 'z'), upward + downward)]
    unnamed x10 -> x18, local copies, waits for them, and re-layouts: 1.28 us -> 6.66 us
    ppermute x8 -> x11, waiting for transfers between devices: 7.15 us -> 4.78 us  [the longest x7 4.77 us: hop(): return lax.ppermute(block, ('core', 'z'), upward + downward)]
    all_to_all x1, blocking collectives: 27.3 us -> 25.7 us  [exchange(): return lax.all_to_all(blocks, axes, 0, 0, tiled=True)]
  transfers between devices with their start and end apart: 10 -> 13, of which waited for: 6 -> 4; matrix products, arithmetic and copies ran while one was open for 7% -> 6% of each run, Pallas kernels for 3% -> 1%
where the time goes in v2:
time: 110 us; the launch traced here: 108 us
  starting transfers between devices  48.5 us (44%)
  blocking collectives  25.7 us (23%)
  waiting for transfers between devices  16.5 us (15%)
  local copies, waits for them, and re-layouts  7.42 us (7%)
  matrix products  7.17 us (7%)
  Pallas kernels  2.7 us (2%)
    ppermute x7, starting transfers between devices, hop(): return lax.ppermute(block, ('core', 'z'), upward + downward)  33.4 us
    all_to_all x1, blocking collectives, exchange(): return lax.all_to_all(blocks, axes, 0, 0, tiled=True)  25.7 us
    all_to_all x2, waiting for transfers between devices, exchange(): return lax.all_to_all(blocks, axes, 0, 0, tiled=True)  11.7 us
    ppermute x4, starting transfers between devices, swap(): return lax.ppermute(block, 'core', [(0, 1), (1, 0)])  7.76 us
    all_to_all x2, starting transfers between devices, exchange(): return lax.all_to_all(blocks, axes, 0, 0, tiled=True)  7.43 us
    dot_general x8, matrix products, product(): return jnp.dot(piece[:tokens], weight, preferred_element_type=f32)  7.17 us
    unnamed x18, local copies, waits for them, and re-layouts  6.66 us
    ppermute x7, waiting for transfers between devices, hop(): return lax.ppermute(block, ('core', 'z'), upward + downward)  4.77 us
  transfers between devices with their start and end apart: 13, of which 4 were waited for; matrix products, arithmetic and copies ran while one was open for 6% of the time, Pallas kernels for 1%

profile of v2, /device:TPU:1, one launch (start us, length us, event | category | flops | bytes accessed | tf_op | source)
XLA Modules:
  0.0 108.4 jit_solution(10678257261595140276)
XLA Ops:
  0.0 0.9 copy-done
  1.0 0.9 copy-done.2
  1.9 0.3 shard_map.73
  2.2 25.7 %all_to_all.15.row = bf16[16,32,128]{2,1,0:T(8,128)(2,1)S(1)} all-to-all(bf16[16,32,128]{2,1,0:T(8,128)(2,1)S(1)} %shard_map.73), channel_id=1, replica_groups=mesh['y'=8,'x'=8,'core'=2,'z'=8] {'x','core'}, dimensions={0} | all-to-all | bytes 262144 | tf_op jit(solution)/shard_map/all_to_all | solution.py:96
  27.9 0.7 shard_map.74
  28.5 3.4 %all-to-all-start.1 = ((bf16[8,32,128]{2,1,0:T(8,128)(2,1)}), bf16[8,32,128]{2,1,0:T(8,128)(2,1)S(1)}, u32[]{:S(2)}, u32[]{:S(2)}) async-start(bf16[8,32,128]{2,1,0:T(8,128)(2,1)} %shard_map.74), calls=%async_computation.1 | async-start | bytes 131072 | tf_op jit(solution)/shard_map/all_to_all | solution.py:96
  31.9 7.7 %all-to-all-done.1.totals = bf16[8,32,128]{2,1,0:T(8,128)(2,1)S(1)} async-done(((bf16[8,32,128]{2,1,0:T(8,128)(2,1)}), bf16[8,32,128]{2,1,0:T(8,128)(2,1)S(1)}, u32[]{:S(2)}, u32[]{:S(2)}) %all-to-all-start.1) | async-done | bytes 65568 | tf_op jit(solution)/shard_map/all_to_all | solution.py:96
  39.6 0.7 shard_map.75
  40.3 4.1 %all-to-all-start.2 = ((bf16[16,32,128]{2,1,0:T(8,128)(2,1)}), bf16[16,32,128]{2,1,0:T(8,128)(2,1)S(1)}, u32[]{:S(2)}, u32[]{:S(2)}) async-start(bf16[16,32,128]{2,1,0:T(8,128)(2,1)} %shard_map.75), calls=%async_computation.2 | async-start | bytes 262144 | tf_op jit(solution)/shard_map/all_to_all | solution.py:96
  44.4 0.8 dynamic_slice.27
  45.2 0.9 copy-done.1
  46.1 0.9 copy-done.3
  47.1 0.9 copy-done.4
  48.0 0.9 copy-done.6
  49.0 0.7 shard_map.76
  49.7 3.9 %all-to-all-done.2 = bf16[16,32,128]{2,1,0:T(8,128)(2,1)S(1)} async-done(((bf16[16,32,128]{2,1,0:T(8,128)(2,1)}), bf16[16,32,128]{2,1,0:T(8,128)(2,1)S(1)}, u32[]{:S(2)}, u32[]{:S(2)}) %all-to-all-start.2) | async-done | bytes 131104 | tf_op jit(solution)/shard_map/all_to_all | solution.py:96
  53.6 0.9 copy-done.5
  54.6 0.4 shard_map.77
  55.0 12.5 %collective-permute-start = (bf16[272,512]{1,0:T(8,128)(2,1)S(1)}, bf16[272,512]{1,0:T(8,128)(2,1)S(1)}, u32[]{:S(2)}, u32[]{:S(2)}) collective-permute-start(bf16[272,512]{1,0:T(8,128)(2,1)S(1)} %shard_map.77), channel_id=1, source_target_pairs={{0,1},{1,2},{2,3},{3,4},{4,5},{5,6},{6,7},{7,0},{8,15},{9,8},{10,9... | collective-permute-start | bytes 835592 | tf_op jit(solution)/shard_map/ppermute | solution.py:102
  67.5 1.9 %collective-permute-start.1 = (bf16[272,512]{1,0:T(8,128)(2,1)S(1)}, bf16[272,512]{1,0:T(8,128)(2,1)S(1)}, u32[]{:S(2)}, u32[]{:S(2)}) collective-permute-start(bf16[272,512]{1,0:T(8,128)(2,1)S(1)} %shard_map.77), channel_id=1, source_target_pairs={{0,8},{8,0},{1,9},{9,1},{2,10},{10,2},{3,11},{11,3},{4,12},{12,4},... | collective-permute-start | bytes 835592 | tf_op jit(solution)/shard_map/ppermute | solution.py:106
  69.5 1.5 %fusion.16 = f32[256,768]{1,0:T(8,128)S(1)} fusion(bf16[4096,768]{1,0:T(8,128)(2,1)} %param.12, s32[]{:T(128)S(6)} %select_n.28, bf16[272,512]{1,0:T(8,128)(2,1)S(1)} %shard_map.77), kind=kOutput, calls=%fused_computation.20 | convolution fusion | flops 201326592 | bytes 1835012 | tf_op jit(solution)/shard_map/dot_general | solution.py:146
  71.0 0.0 collective-permute-done
  71.0 5.0 %collective-permute-start.4 = (bf16[272,512]{1,0:T(8,128)(2,1)S(1)}, bf16[272,512]{1,0:T(8,128)(2,1)S(1)}, u32[]{:S(2)}, u32[]{:S(2)}) collective-permute-start(bf16[272,512]{1,0:T(8,128)(2,1)S(1)} %collective-permute-done), channel_id=1, source_target_pairs={{0,1},{1,2},{2,3},{3,4},{4,5},{5,6},{6,7},{7,0},{8,15},{9,8},{10,9... | collective-permute-start | bytes 835592 | tf_op jit(solution)/shard_map/ppermute | solution.py:102
  76.0 0.0 collective-permute-done.1
  76.0 1.9 %collective-permute-start.2 = (bf16[272,512]{1,0:T(8,128)(2,1)S(1)}, bf16[272,512]{1,0:T(8,128)(2,1)S(1)}, u32[]{:S(2)}, u32[]{:S(2)}) collective-permute-start(bf16[272,512]{1,0:T(8,128)(2,1)S(1)} %collective-permute-done.1), channel_id=1, source_target_pairs={{0,1},{1,2},{2,3},{3,4},{4,5},{5,6},{6,7},{7,0},{8,15},{9,8},{10,9... | collective-permute-start | bytes 835592 | tf_op jit(solution)/shard_map/ppermute | solution.py:102
  78.0 1.5 %convolution_add_fusion.3 = f32[256,768]{1,0:T(8,128)S(1)} fusion(f32[256,768]{1,0:T(8,128)S(1)} %fusion.16, bf16[4096,768]{1,0:T(8,128)(2,1)} %param.12, s32[]{:T(128)S(6)} %select_n.29, bf16[272,512]{1,0:T(8,128)(2,1)S(1)} %collective-permute-done), kind=kOutput, calls=%fused_computation.8 | convolution fusion | flops 201523200 | bytes 2621444 | tf_op jit(solution)/shard_map/dot_general | solution.py:146
  79.5 0.0 copy-start.8
  79.5 4.1 %collective-permute-done.2 = bf16[272,512]{1,0:T(8,128)(2,1)S(1)} collective-permute-done((bf16[272,512]{1,0:T(8,128)(2,1)S(1)}, bf16[272,512]{1,0:T(8,128)(2,1)S(1)}, u32[]{:S(2)}, u32[]{:S(2)}) %collective-permute-start.2) | collective-permute-done | bytes 278560 | tf_op jit(solution)/shard_map/ppermute | solution.py:102
  83.6 3.9 %collective-permute-start.5 = (bf16[272,512]{1,0:T(8,128)(2,1)S(1)}, bf16[272,512]{1,0:T(8,128)(2,1)S(1)}, u32[]{:S(2)}, u32[]{:S(2)}) collective-permute-start(bf16[272,512]{1,0:T(8,128)(2,1)S(1)} %collective-permute-done.2), channel_id=1, source_target_pairs={{0,1},{1,2},{2,3},{3,4},{4,5},{5,6},{6,7},{7,0},{8,15},{9,8},{10,9... | collective-permute-start | bytes 835592 | tf_op jit(solution)/shard_map/ppermute | solution.py:102
  87.5 1.9 %collective-permute-start.3 = (bf16[272,512]{1,0:T(8,128)(2,1)S(1)}, bf16[272,512]{1,0:T(8,128)(2,1)S(1)}, u32[]{:S(2)}, u32[]{:S(2)}) collective-permute-start(bf16[272,512]{1,0:T(8,128)(2,1)S(1)} %collective-permute-done.2), channel_id=1, source_target_pairs={{0,8},{8,0},{1,9},{9,1},{2,10},{10,2},{3,11},{11,3},{4,12},{12,4},... | collective-permute-start | bytes 835592 | tf_op jit(solution)/shard_map/ppermute | solution.py:106
  89.4 0.0 collective-permute-done.4
  89.4 3.9 %collective-permute-start.7 = (bf16[272,512]{1,0:T(8,128)(2,1)S(1)}, bf16[272,512]{1,0:T(8,128)(2,1)S(1)}, u32[]{:S(2)}, u32[]{:S(2)}) collective-permute-start(bf16[272,512]{1,0:T(8,128)(2,1)S(1)} %collective-permute-done.4), channel_id=1, source_target_pairs={{0,1},{1,2},{2,3},{3,4},{4,5},{5,6},{6,7},{7,0},{8,15},{9,8},{10,9... | collective-permute-start | bytes 835592 | tf_op jit(solution)/shard_map/ppermute | solution.py:102
  93.3 1.5 %fusion.12 = f32[256,768]{1,0:T(8,128)S(1)} fusion(bf16[4096,768]{1,0:T(8,128)(2,1)} %param.12, s32[]{:T(128)S(6)} %select_n.31, bf16[272,512]{1,0:T(8,128)(2,1)S(1)} %collective-permute-done.4), kind=kOutput, calls=%fused_computation.16 | convolution fusion | flops 201326592 | bytes 1835012 | tf_op jit(solution)/shard_map/dot_general | solution.py:146
  94.8 0.0 collective-permute-done.5
  94.8 1.9 %collective-permute-start.8 = (bf16[272,512]{1,0:T(8,128)(2,1)S(1)}, bf16[272,512]{1,0:T(8,128)(2,1)S(1)}, u32[]{:S(2)}, u32[]{:S(2)}) collective-permute-start(bf16[272,512]{1,0:T(8,128)(2,1)S(1)} %collective-permute-done.5), channel_id=1, source_target_pairs={{0,1},{1,2},{2,3},{3,4},{4,5},{5,6},{6,7},{7,0},{8,15},{9,8},{10,9... | collective-permute-start | bytes 835592 | tf_op jit(solution)/shard_map/ppermute | solution.py:102
  96.8 1.9 %collective-permute-start.6 = (bf16[272,512]{1,0:T(8,128)(2,1)S(1)}, bf16[272,512]{1,0:T(8,128)(2,1)S(1)}, u32[]{:S(2)}, u32[]{:S(2)}) collective-permute-start(bf16[272,512]{1,0:T(8,128)(2,1)S(1)} %collective-permute-done.5), channel_id=1, source_target_pairs={{0,8},{8,0},{1,9},{9,1},{2,10},{10,2},{3,11},{11,3},{4,12},{12,4},... | collective-permute-start | bytes 835592 | tf_op jit(solution)/shard_map/ppermute | solution.py:106
  98.7 4.2 %collective-permute-start.10 = (bf16[272,512]{1,0:T(8,128)(2,1)S(1)}, bf16[272,512]{1,0:T(8,128)(2,1)S(1)}, u32[]{:S(2)}, u32[]{:S(2)}) collective-permute-start(bf16[272,512]{1,0:T(8,128)(2,1)S(1)} %collective-permute-done.7), channel_id=1, source_target_pairs={{0,1},{1,2},{2,3},{3,4},{4,5},{5,6},{6,7},{7,0},{8,15},{9,8},{10,9... | collective-permute-start | bytes 835592 | tf_op jit(solution)/shard_map/ppermute | solution.py:102
  102.9 0.0 collective-permute-done.3
  103.0 0.4 fusion.4
  103.3 0.4 fusion.9
  103.8 0.0 collective-permute-done.8
  103.8 2.0 %collective-permute-start.9 = (bf16[272,512]{1,0:T(8,128)(2,1)S(1)}, bf16[272,512]{1,0:T(8,128)(2,1)S(1)}, u32[]{:S(2)}, u32[]{:S(2)}) collective-permute-start(bf16[272,512]{1,0:T(8,128)(2,1)S(1)} %collective-permute-done.8), channel_id=1, source_target_pairs={{0,8},{8,0},{1,9},{9,1},{2,10},{10,2},{3,11},{11,3},{4,12},{12,4},... | collective-permute-start | bytes 835592 | tf_op jit(solution)/shard_map/ppermute | solution.py:106
  105.8 0.6 collective-permute-done.10
  106.4 0.0 collective-permute-done.6
  106.4 0.4 fusion.6
  106.8 0.4 fusion.3
  107.2 0.0 collective-permute-done.9
  107.3 1.2 %fusion.5 = bf16[256,768]{1,0:T(8,128)(2,1)} fusion(f32[256,768]{1,0:T(8,128)S(1)} %fusion.6, f32[256,768]{1,0:T(8,128)S(1)} %fusion.3, bf16[256,768]{1,0:T(8,128)(2,1)S(1)} %copy-done.8, bf16[4096,768]{1,0:T(8,128)(2,1)S(1)} %copy-done.7, s32[]{:T(128)S(6)} %select_n.34, f32[256]{0:T(256)S(1)} %add_rsqrt_fusion, bf16[272,512]{1,0:T(8,128)(2,1)S(1)} %collective-permute-done.9), kind=kOutput, calls=%fused_computation.9 | convolution fusion | flops 202506240 | bytes 3408900 | tf_op jit(solution)/shard_map/dot_general | solution.py:146
  (20 shorter events, 0.2 us)
Async XLA Ops:
  0.0 0.9 copy-start
  1.0 0.9 copy-start.2
  28.5 11.1 %all-to-all-start.1 = ((bf16[8,32,128]{2,1,0:T(8,128)(2,1)}), bf16[8,32,128]{2,1,0:T(8,128)(2,1)S(1)}, u32[]{:S(2)}, u32[]{:S(2)}) async-start(bf16[8,32,128]{2,1,0:T(8,128)(2,1)} %shard_map.74), calls=%async_computation.1 | async-start | bytes 131072 | tf_op jit(solution)/shard_map/all_to_all | solution.py:96
  40.3 13.3 %all-to-all-start.2 = ((bf16[16,32,128]{2,1,0:T(8,128)(2,1)}), bf16[16,32,128]{2,1,0:T(8,128)(2,1)S(1)}, u32[]{:S(2)}, u32[]{:S(2)}) async-start(bf16[16,32,128]{2,1,0:T(8,128)(2,1)} %shard_map.75), calls=%async_computation.2 | async-start | bytes 262144 | tf_op jit(solution)/shard_map/all_to_all | solution.py:96
  45.2 0.9 copy-start.1
  46.1 0.9 copy-start.3
  47.1 0.9 copy-start.4
  48.0 0.9 copy-start.6
  53.6 1.0 copy-start.5
  54.6 48.4 %copy-start.7 = (bf16[4096,768]{1,0:T(8,128)(2,1)S(1)}, bf16[4096,768]{1,0:T(8,128)(2,1)}, u32[]{:S(2)}) copy-start(bf16[4096,768]{1,0:T(8,128)(2,1)} %param.12) | copy-start | bytes 18874372
  55.0 16.0 %collective-permute-start = (bf16[272,512]{1,0:T(8,128)(2,1)S(1)}, bf16[272,512]{1,0:T(8,128)(2,1)S(1)}, u32[]{:S(2)}, u32[]{:S(2)}) collective-permute-start(bf16[272,512]{1,0:T(8,128)(2,1)S(1)} %shard_map.77), channel_id=1, source_target_pairs={{0,1},{1,2},{2,3},{3,4},{4,5},{5,6},{6,7},{7,0},{8,15},{9,8},{10,9... | collective-permute-start | bytes 835592 | tf_op jit(solution)/shard_map/ppermute | solution.py:102
  67.5 8.5 %collective-permute-start.1 = (bf16[272,512]{1,0:T(8,128)(2,1)S(1)}, bf16[272,512]{1,0:T(8,128)(2,1)S(1)}, u32[]{:S(2)}, u32[]{:S(2)}) collective-permute-start(bf16[272,512]{1,0:T(8,128)(2,1)S(1)} %shard_map.77), channel_id=1, source_target_pairs={{0,8},{8,0},{1,9},{9,1},{2,10},{10,2},{3,11},{11,3},{4,12},{12,4},... | collective-permute-start | bytes 835592 | tf_op jit(solution)/shard_map/ppermute | solution.py:106
  71.0 18.4 %collective-permute-start.4 = (bf16[272,512]{1,0:T(8,128)(2,1)S(1)}, bf16[272,512]{1,0:T(8,128)(2,1)S(1)}, u32[]{:S(2)}, u32[]{:S(2)}) collective-permute-start(bf16[272,512]{1,0:T(8,128)(2,1)S(1)} %collective-permute-done), channel_id=1, source_target_pairs={{0,1},{1,2},{2,3},{3,4},{4,5},{5,6},{6,7},{7,0},{8,15},{9,8},{10,9... | collective-permute-start | bytes 835592 | tf_op jit(solution)/shard_map/ppermute | solution.py:102
  76.0 7.6 %collective-permute-start.2 = (bf16[272,512]{1,0:T(8,128)(2,1)S(1)}, bf16[272,512]{1,0:T(8,128)(2,1)S(1)}, u32[]{:S(2)}, u32[]{:S(2)}) collective-permute-start(bf16[272,512]{1,0:T(8,128)(2,1)S(1)} %collective-permute-done.1), channel_id=1, source_target_pairs={{0,1},{1,2},{2,3},{3,4},{4,5},{5,6},{6,7},{7,0},{8,15},{9,8},{10,9... | collective-permute-start | bytes 835592 | tf_op jit(solution)/shard_map/ppermute | solution.py:102
  79.5 27.8 %copy-start.8 = (bf16[256,768]{1,0:T(8,128)(2,1)S(1)}, bf16[256,768]{1,0:T(8,128)(2,1)}, u32[]{:S(2)}) copy-start(bf16[256,768]{1,0:T(8,128)(2,1)} %param.13) | copy-start | bytes 1179652
  83.6 11.2 %collective-permute-start.5 = (bf16[272,512]{1,0:T(8,128)(2,1)S(1)}, bf16[272,512]{1,0:T(8,128)(2,1)S(1)}, u32[]{:S(2)}, u32[]{:S(2)}) collective-permute-start(bf16[272,512]{1,0:T(8,128)(2,1)S(1)} %collective-permute-done.2), channel_id=1, source_target_pairs={{0,1},{1,2},{2,3},{3,4},{4,5},{5,6},{6,7},{7,0},{8,15},{9,8},{10,9... | collective-permute-start | bytes 835592 | tf_op jit(solution)/shard_map/ppermute | solution.py:102
  87.5 15.4 %collective-permute-start.3 = (bf16[272,512]{1,0:T(8,128)(2,1)S(1)}, bf16[272,512]{1,0:T(8,128)(2,1)S(1)}, u32[]{:S(2)}, u32[]{:S(2)}) collective-permute-start(bf16[272,512]{1,0:T(8,128)(2,1)S(1)} %collective-permute-done.2), channel_id=1, source_target_pairs={{0,8},{8,0},{1,9},{9,1},{2,10},{10,2},{3,11},{11,3},{4,12},{12,4},... | collective-permute-start | bytes 835592 | tf_op jit(solution)/shard_map/ppermute | solution.py:106
  89.4 9.3 %collective-permute-start.7 = (bf16[272,512]{1,0:T(8,128)(2,1)S(1)}, bf16[272,512]{1,0:T(8,128)(2,1)S(1)}, u32[]{:S(2)}, u32[]{:S(2)}) collective-permute-start(bf16[272,512]{1,0:T(8,128)(2,1)S(1)} %collective-permute-done.4), channel_id=1, source_target_pairs={{0,1},{1,2},{2,3},{3,4},{4,5},{5,6},{6,7},{7,0},{8,15},{9,8},{10,9... | collective-permute-start | bytes 835592 | tf_op jit(solution)/shard_map/ppermute | solution.py:102
  94.8 8.9 %collective-permute-start.8 = (bf16[272,512]{1,0:T(8,128)(2,1)S(1)}, bf16[272,512]{1,0:T(8,128)(2,1)S(1)}, u32[]{:S(2)}, u32[]{:S(2)}) collective-permute-start(bf16[272,512]{1,0:T(8,128)(2,1)S(1)} %collective-permute-done.5), channel_id=1, source_target_pairs={{0,1},{1,2},{2,3},{3,4},{4,5},{5,6},{6,7},{7,0},{8,15},{9,8},{10,9... | collective-permute-start | bytes 835592 | tf_op jit(solution)/shard_map/ppermute | solution.py:102
  96.8 9.7 %collective-permute-start.6 = (bf16[272,512]{1,0:T(8,128)(2,1)S(1)}, bf16[272,512]{1,0:T(8,128)(2,1)S(1)}, u32[]{:S(2)}, u32[]{:S(2)}) collective-permute-start(bf16[272,512]{1,0:T(8,128)(2,1)S(1)} %collective-permute-done.5), channel_id=1, source_target_pairs={{0,8},{8,0},{1,9},{9,1},{2,10},{10,2},{3,11},{11,3},{4,12},{12,4},... | collective-permute-start | bytes 835592 | tf_op jit(solution)/shard_map/ppermute | solution.py:106
  98.7 7.7 %collective-permute-start.10 = (bf16[272,512]{1,0:T(8,128)(2,1)S(1)}, bf16[272,512]{1,0:T(8,128)(2,1)S(1)}, u32[]{:S(2)}, u32[]{:S(2)}) collective-permute-start(bf16[272,512]{1,0:T(8,128)(2,1)S(1)} %collective-permute-done.7), channel_id=1, source_target_pairs={{0,1},{1,2},{2,3},{3,4},{4,5},{5,6},{6,7},{7,0},{8,15},{9,8},{10,9... | collective-permute-start | bytes 835592 | tf_op jit(solution)/shard_map/ppermute | solution.py:102
  103.8 3.5 %collective-permute-start.9 = (bf16[272,512]{1,0:T(8,128)(2,1)S(1)}, bf16[272,512]{1,0:T(8,128)(2,1)S(1)}, u32[]{:S(2)}, u32[]{:S(2)}) collective-permute-start(bf16[272,512]{1,0:T(8,128)(2,1)S(1)} %collective-permute-done.8), channel_id=1, source_target_pairs={{0,8},{8,0},{1,9},{9,1},{2,10},{10,2},{3,11},{11,3},{4,12},{12,4},... | collective-permute-start | bytes 835592 | tf_op jit(solution)/shard_map/ppermute | solution.py:106

commit v3 on v1

--- a/solution.py
+++ b/solution.py
@@ -10,20 +10,25 @@
 INNER = 4096
 SIDE = 8
 CORES = 2
+LIMIT = 12 * 2**20
 
 epsilon = 1e-06
 f32 = jnp.float32
 bf16 = jnp.bfloat16
 
 
-def call(kernel, out_shape, *args, flops=0, smem=0):
+VMEM = pl.BlockSpec(memory_space=pltpu.VMEM)
+SMEM = pl.BlockSpec(memory_space=pltpu.SMEM)
+
+
+def call(kernel, out_shape, specs, args, flops=0):
     size = sum(a.size * a.dtype.itemsize for a in args)
     return pl.pallas_call(
         kernel,
         out_shape=out_shape,
-        in_specs=[pl.BlockSpec(memory_space=pltpu.SMEM)] * smem
-        + [pl.BlockSpec(memory_space=pltpu.VMEM)] * (len(args) - smem),
-        out_specs=jax.tree.map(lambda _: pl.BlockSpec(memory_space=pltpu.VMEM), out_shape),
+        in_specs=specs,
+        out_specs=jax.tree.map(lambda _: VMEM, out_shape),
+        compiler_params=pltpu.CompilerParams(vmem_limit_bytes=LIMIT),
         cost_estimate=pl.CostEstimate(flops=flops, bytes_accessed=size, transcendentals=0),
     )(*args)
 
@@ -59,7 +64,7 @@
         run = run + row[member].astype(f32)
 
 
-def local_kernel(queries, keys, values, gates, gain, local, gated):
+def local_kernel(queries, keys, values, local, queries_kept):
     tokens = queries.shape[0]
     later = lax.broadcasted_iota(jnp.int32, (tokens, tokens), 0)
     earlier = lax.broadcasted_iota(jnp.int32, (tokens, tokens), 1)
@@ -69,7 +74,14 @@
         )
         scores = jnp.where(earlier <= later, scores, 0.0).astype(bf16)
         local[:, cols] = jnp.dot(scores, values[:, cols], preferred_element_type=f32)
-    gated[...] = gain[...] * jax.nn.sigmoid(gates[...].astype(f32))
+    queries_kept[...] = queries[...]
+
+
+def gate_kernel(place, gain, gates, gated):
+    groups = heads_of(gates)
+    for h, cols in enumerate(groups):
+        gain_row = gain[pl.ds(place[0] * len(groups) + h, 1), :]
+        gated[:, cols] = gain_row * jax.nn.sigmoid(gates[:, cols].astype(f32))
 
 
 def attend_kernel(queries, state, local, gated, out):
@@ -94,9 +106,54 @@
     return lax.all_to_all(blocks, axes, 0, 0, tiled=True)
 
 
+def ring(block, sign):
+    pairs = [(z, (z + sign) % SIDE) for z in range(SIDE)]
+    pairs += [(SIDE + z, SIDE + (z - sign) % SIDE) for z in range(SIDE)]
+    return lax.ppermute(block, ("core", "z"), pairs)
+
+
 def shift(block, hops):
-    pairs = [(place, (place + hops) % SIDE) for place in range(SIDE)]
-    return lax.ppermute(block, "z", pairs)
+    return lax.ppermute(block, "z", [(z, (z + hops) % SIDE) for z in range(SIDE)])
+
+
+def gather_seven(block, tokens):
+    one = two = block
+    pieces = [(block, 0)]
+    for step in range(1, SIDE // 2):
+        one, two = ring(one, 1), ring(two, -1)
+        pieces += [(one, step), (two, -step)]
+    pieces.append((ring(one, 1), SIDE // 2))
+    behind = 2 * lax.axis_index("core") - 1
+    return [(piece, offset * behind) for piece, offset in pieces]
+
+
+def gather_three(block, tokens):
+    half = tokens // 2
+    up1, down1 = shift(block, -1), shift(block, 1)
+    up2, down2 = shift(up1, -1), shift(down1, 1)
+    block, up1, down1, up2, down2 = lax.optimization_barrier((block, up1, down1, up2, down2))
+    up3, down3 = shift(up2, -1), shift(down2, 1)
+    far = jnp.concatenate([shift(up2[:half], -2), shift(down2[half:], 2)], axis=0)
+    return [(block, 0), (up1, 1), (down1, -1), (up2, 2), (down2, -2), (up3, 3), (down3, -3), (far, 4)]
+
+
+def finish(pieces, weight, residual):
+    tokens = residual.shape[0]
+    z = lax.axis_index("z")
+    total = jnp.zeros((tokens,), f32)
+    projected = None
+    for piece, offset in pieces:
+        width = piece.shape[1]
+        source = lax.rem(z + offset + SIDE, SIDE)
+        rows = lax.dynamic_slice_in_dim(weight, source * width, width, 0)
+        part = jnp.dot(piece[:tokens], rows, preferred_element_type=f32)
+        total = total + jnp.sum(piece[tokens : tokens + 3, :tokens].astype(f32), axis=0)
+        projected = part if projected is None else projected + part
+    scale_rows = lax.rsqrt(total / INNER + epsilon)
+    return (projected * scale_rows[:, None] + residual.astype(f32)).astype(bf16)
+
+
+gather = gather_three
 
 
 def on_device(queries, keys, values, gate_logits, norm_gain, out_weight, residual):
@@ -104,55 +161,37 @@
     heads = width // HEAD_DIM
     row_places = SIDE * CORES
     rows = heads * HEAD_DIM // row_places
-    z = lax.axis_index("z")
     shape = jax.ShapeDtypeStruct
+    tile = shape((tokens, width), bf16)
+    wide = shape((tokens, width), f32)
+    chunk = shape((row_places, rows, HEAD_DIM), bf16)
 
     own = call(
-        state_kernel, shape((row_places, rows, HEAD_DIM), bf16), keys, values,
-        flops=2 * tokens * width * HEAD_DIM,
+        state_kernel, chunk, [VMEM] * 2, (keys, values), flops=2 * tokens * width * HEAD_DIM
     )
     row = exchange(own, ("x", "core"))
-    totals = call(total_kernel, shape((SIDE, rows, HEAD_DIM), bf16), row)
+    totals = call(total_kernel, shape((SIDE, rows, HEAD_DIM), bf16), [VMEM], (row,))
+    totals, queries = lax.optimization_barrier((totals, queries))
     totals = exchange(totals, "y")
-    place = lax.axis_index("y").reshape(1)
-    state = call(
-        prefix_kernel, shape((row_places, rows, HEAD_DIM), bf16), place, row, totals, smem=1
-    )
+    local, queries = call(
+        local_kernel, [wide, tile], [VMEM] * 3, (queries, keys, values),
+        flops=4 * tokens * tokens * width,
+    )
+    y_place = lax.axis_index("y").reshape(1)
+    totals, local = lax.optimization_barrier((totals, local))
+    state = call(prefix_kernel, chunk, [SMEM, VMEM, VMEM], (y_place, row, totals))
+    state, gate_logits = lax.optimization_barrier((state, gate_logits))
     state = exchange(state, ("x", "core")).reshape(heads, HEAD_DIM, HEAD_DIM)
-
-    gain_here = lax.dynamic_slice_in_dim(norm_gain, z * width, width, 0)[None]
-    local, gated = call(
-        local_kernel, [shape((tokens, width), f32)] * 2,
-        queries, keys, values, gate_logits, gain_here,
-        flops=4 * tokens * tokens * width,
+    z_place = lax.axis_index("z").reshape(1)
+    gated = call(
+        gate_kernel, wide, [SMEM, VMEM, VMEM],
+        (z_place, norm_gain.reshape(-1, HEAD_DIM), gate_logits), flops=tokens * width,
     )
     block = call(
-        attend_kernel, shape((tokens + 16, width), bf16), queries, state, local, gated,
-        flops=2 * tokens * width * HEAD_DIM,
-    )
-
-    def product(piece, offset):
-        source = lax.rem(z + offset + SIDE, SIDE)
-        weight = lax.dynamic_slice_in_dim(out_weight, source * width, width, 0)
-        return jnp.dot(piece[:tokens], weight, preferred_element_type=f32)
-
-    def squares(piece):
-        return jnp.sum(piece[tokens : tokens + 3, :tokens].astype(f32), axis=0)
-
-    half = tokens // 2
-    up1, down1 = shift(block, -1), shift(block, 1)
-    up2, down2 = shift(up1, -1), shift(down1, 1)
-    up3, down3 = shift(up2, -1), shift(down2, 1)
-    far = jnp.concatenate([shift(up2[:half], -2), shift(down2[half:], 2)], axis=0)
-    pieces = [(block, 0), (up1, 1), (down1, -1), (up2, 2), (down2, -2), (up3, 3), (down3, -3), (far, 4)]
-    total = jnp.zeros((tokens,), f32)
-    projected = None
-    for piece, offset in pieces:
-        total = total + squares(piece)
-        part = product(piece, offset)
-        projected = part if projected is None else projected + part
-    scale_rows = lax.rsqrt(total / INNER + epsilon)
-    return (projected * scale_rows[:, None] + residual.astype(f32)).astype(bf16)
+        attend_kernel, shape((tokens + 16, width), bf16), [VMEM] * 4,
+        (queries, state, local, gated), flops=2 * tokens * width * HEAD_DIM,
+    )
+    return finish(gather(block, tokens), out_weight, residual)
 
 
 def solution(mesh):

time: 111 us -> 111 us (level)
  Pallas kernels: 10.6 us -> 2.75 us
  waiting for transfers between devices: 19.9 us -> 24.6 us
  local copies, waits for them, and re-layouts: 2.64 us -> 6.44 us
  blocking collectives: 27.3 us -> 25.7 us
  starting transfers between devices: 41.2 us -> 42.7 us
    pallas_call x5 -> x6, Pallas kernels: 10.6 us -> 2.75 us  [call(): pl.pallas_call(kernel, out_shape=out_shape, in_specs=specs, out_specs=jax...]
    ppermute x8, waiting for transfers between devices: 7.15 us -> 13 us  [shift(): lax.ppermute(block, 'z', [(z, (z + hops) % SIDE) for z in range(SIDE)])]
    unnamed x10 -> x18, local copies, waits for them, and re-layouts: 1.28 us -> 6.42 us
    all_to_all x1, blocking collectives: 27.3 us -> 25.7 us  [exchange(): return lax.all_to_all(blocks, axes, 0, 0, tiled=True)]
    ppermute x8, starting transfers between devices: 33.7 us -> 35.3 us  [shift(): lax.ppermute(block, 'z', [(z, (z + hops) % SIDE) for z in range(SIDE)])]
    dynamic_slice x1 -> x0, local copies, waits for them, and re-layouts: 1.35 us -> none  [on_device(): gain_here = lax.dynamic_slice_in_dim(norm_gain, z * width, width, 0)[None]]
  transfers between devices with their start and end apart: 10 -> 10, of which waited for: 6 -> 5; matrix products, arithmetic and copies ran while one was open for 7% -> 5% of each run, Pallas kernels for 3% -> 1%
where the time goes in v3:
time: 111 us; the launch traced here: 110 us
  starting transfers between devices  42.7 us (38%)
  blocking collectives  25.7 us (23%)
  waiting for transfers between devices  24.6 us (22%)
  matrix products  7.25 us (7%)
  local copies, waits for them, and re-layouts  6.44 us (6%)
  Pallas kernels  2.75 us (2%)
    ppermute x8, starting transfers between devices, shift(): lax.ppermute(block, 'z', [(z, (z + hops) % SIDE) for z in range(SIDE)])  35.3 us
    all_to_all x1, blocking collectives, exchange(): return lax.all_to_all(blocks, axes, 0, 0, tiled=True)  25.7 us
    ppermute x8, waiting for transfers between devices, shift(): lax.ppermute(block, 'z', [(z, (z + hops) % SIDE) for z in range(SIDE)])  13 us
    all_to_all x2, waiting for transfers between devices, exchange(): return lax.all_to_all(blocks, axes, 0, 0, tiled=True)  11.7 us
    all_to_all x2, starting transfers between devices, exchange(): return lax.all_to_all(blocks, axes, 0, 0, tiled=True)  7.43 us
    dot_general x8, matrix products, finish(): part = jnp.dot(piece[:tokens], rows, preferred_element_type=f32)  7.25 us
    unnamed x18, local copies, waits for them, and re-layouts  6.42 us
    pallas_call x6, Pallas kernels, call(): pl.pallas_call(kernel, out_shape=out_shape, in_specs=specs, out_specs=jax...  2.75 us
  transfers between devices with their start and end apart: 10, of which 5 were waited for; matrix products, arithmetic and copies ran while one was open for 5% of the time, Pallas kernels for 1%

profile of v3, /device:TPU:1, one launch (start us, length us, event | category | flops | bytes accessed | tf_op | source)
XLA Modules:
  0.0 110.0 jit_solution(8711398507418288538)
XLA Ops:
  0.0 0.0 copy-start
  0.0 0.9 copy-done
  1.0 0.9 copy-done.2
  1.9 0.3 shard_map.73
  2.2 25.7 %all_to_all.15.row = bf16[16,32,128]{2,1,0:T(8,128)(2,1)S(1)} all-to-all(bf16[16,32,128]{2,1,0:T(8,128)(2,1)S(1)} %shard_map.73), channel_id=1, replica_groups=mesh['y'=8,'x'=8,'core'=2,'z'=8] {'x','core'}, dimensions={0} | all-to-all | bytes 262144 | tf_op jit(solution)/shard_map/all_to_all | solution.py:106
  27.9 0.7 shard_map.74
  28.5 3.4 %all-to-all-start.1 = ((bf16[8,32,128]{2,1,0:T(8,128)(2,1)}), bf16[8,32,128]{2,1,0:T(8,128)(2,1)S(1)}, u32[]{:S(2)}, u32[]{:S(2)}) async-start(bf16[8,32,128]{2,1,0:T(8,128)(2,1)} %shard_map.74), calls=%async_computation.1 | async-start | bytes 131072 | tf_op jit(solution)/shard_map/all_to_all | solution.py:106
  31.9 0.0 copy-start.1
  31.9 0.9 copy-done.1
  32.9 0.9 copy-done.3
  33.8 0.9 copy-done.4
  34.8 0.7 shard_map.75
  35.4 4.2 %all-to-all-done.1.totals = bf16[8,32,128]{2,1,0:T(8,128)(2,1)S(1)} async-done(((bf16[8,32,128]{2,1,0:T(8,128)(2,1)}), bf16[8,32,128]{2,1,0:T(8,128)(2,1)S(1)}, u32[]{:S(2)}, u32[]{:S(2)}) %all-to-all-start.1) | async-done | bytes 65568 | tf_op jit(solution)/shard_map/all_to_all | solution.py:106
  39.6 0.7 shard_map.76
  40.3 4.1 %all-to-all-start.2 = ((bf16[16,32,128]{2,1,0:T(8,128)(2,1)}), bf16[16,32,128]{2,1,0:T(8,128)(2,1)S(1)}, u32[]{:S(2)}, u32[]{:S(2)}) async-start(bf16[16,32,128]{2,1,0:T(8,128)(2,1)} %shard_map.76), calls=%async_computation.2 | async-start | bytes 262144 | tf_op jit(solution)/shard_map/all_to_all | solution.py:106
  44.4 0.9 copy-done.5
  45.4 0.7 copy-done.6
  46.1 0.1 shard_map.77.gated
  46.2 7.4 %all-to-all-done.2 = bf16[16,32,128]{2,1,0:T(8,128)(2,1)S(1)} async-done(((bf16[16,32,128]{2,1,0:T(8,128)(2,1)}), bf16[16,32,128]{2,1,0:T(8,128)(2,1)S(1)}, u32[]{:S(2)}, u32[]{:S(2)}) %all-to-all-start.2) | async-done | bytes 131104 | tf_op jit(solution)/shard_map/all_to_all | solution.py:106
  53.6 0.4 shard_map.78
  54.0 12.3 %collective-permute-start = (bf16[272,512]{1,0:T(8,128)(2,1)S(1)}, bf16[272,512]{1,0:T(8,128)(2,1)S(1)}, u32[]{:S(2)}, u32[]{:S(2)}) collective-permute-start(bf16[272,512]{1,0:T(8,128)(2,1)S(1)} %shard_map.78), channel_id=1, source_target_pairs={{0,7},{1,0},{2,1},{3,2},{4,3},{5,4},{6,5},{7,6},{8,15},{9,8},{10,9... | collective-permute-start | bytes 835592 | tf_op jit(solution)/shard_map/ppermute | solution.py:116
  66.3 1.9 %collective-permute-start.1 = (bf16[272,512]{1,0:T(8,128)(2,1)S(1)}, bf16[272,512]{1,0:T(8,128)(2,1)S(1)}, u32[]{:S(2)}, u32[]{:S(2)}) collective-permute-start(bf16[272,512]{1,0:T(8,128)(2,1)S(1)} %shard_map.78), channel_id=1, source_target_pairs={{0,1},{1,2},{2,3},{3,4},{4,5},{5,6},{6,7},{7,0},{8,9},{9,10},{10,1... | collective-permute-start | bytes 835592 | tf_op jit(solution)/shard_map/ppermute | solution.py:116
  68.2 4.4 %collective-permute-done = bf16[272,512]{1,0:T(8,128)(2,1)S(1)} collective-permute-done((bf16[272,512]{1,0:T(8,128)(2,1)S(1)}, bf16[272,512]{1,0:T(8,128)(2,1)S(1)}, u32[]{:S(2)}, u32[]{:S(2)}) %collective-permute-start) | collective-permute-done | bytes 278560 | tf_op jit(solution)/shard_map/ppermute | solution.py:116
  72.6 5.3 %collective-permute-start.2 = (bf16[272,512]{1,0:T(8,128)(2,1)S(1)}, bf16[272,512]{1,0:T(8,128)(2,1)S(1)}, u32[]{:S(2)}, u32[]{:S(2)}) collective-permute-start(bf16[272,512]{1,0:T(8,128)(2,1)S(1)} %collective-permute-done), channel_id=1, source_target_pairs={{0,7},{1,0},{2,1},{3,2},{4,3},{5,4},{6,5},{7,6},{8,15},{9,8},{10,9... | collective-permute-start | bytes 835592 | tf_op jit(solution)/shard_map/ppermute | solution.py:116
  78.0 0.0 collective-permute-done.1
  78.0 1.9 %collective-permute-start.3 = (bf16[272,512]{1,0:T(8,128)(2,1)S(1)}, bf16[272,512]{1,0:T(8,128)(2,1)S(1)}, u32[]{:S(2)}, u32[]{:S(2)}) collective-permute-start(bf16[272,512]{1,0:T(8,128)(2,1)S(1)} %collective-permute-done.1), channel_id=1, source_target_pairs={{0,1},{1,2},{2,3},{3,4},{4,5},{5,6},{6,7},{7,0},{8,9},{9,10},{10,1... | collective-permute-start | bytes 835592 | tf_op jit(solution)/shard_map/ppermute | solution.py:116
  79.9 0.0 copy-start.7
  80.0 3.5 %collective-permute-done.2 = bf16[272,512]{1,0:T(8,128)(2,1)S(1)} collective-permute-done((bf16[272,512]{1,0:T(8,128)(2,1)S(1)}, bf16[272,512]{1,0:T(8,128)(2,1)S(1)}, u32[]{:S(2)}, u32[]{:S(2)}) %collective-permute-start.2) | collective-permute-done | bytes 278560 | tf_op jit(solution)/shard_map/ppermute | solution.py:116
  83.4 5.1 %collective-permute-done.3 = bf16[272,512]{1,0:T(8,128)(2,1)S(1)} collective-permute-done((bf16[272,512]{1,0:T(8,128)(2,1)S(1)}, bf16[272,512]{1,0:T(8,128)(2,1)S(1)}, u32[]{:S(2)}, u32[]{:S(2)}) %collective-permute-start.3) | collective-permute-done | bytes 278560 | tf_op jit(solution)/shard_map/ppermute | solution.py:116
  88.5 1.9 %collective-permute-start.5 = (bf16[272,512]{1,0:T(8,128)(2,1)S(1)}, bf16[272,512]{1,0:T(8,128)(2,1)S(1)}, u32[]{:S(2)}, u32[]{:S(2)}) collective-permute-start(bf16[272,512]{1,0:T(8,128)(2,1)S(1)} %collective-permute-done.3), channel_id=1, source_target_pairs={{0,1},{1,2},{2,3},{3,4},{4,5},{5,6},{6,7},{7,0},{8,9},{9,10},{10,1... | collective-permute-start | bytes 835592 | tf_op jit(solution)/shard_map/ppermute | solution.py:116
  90.5 4.6 %collective-permute-start.4 = (bf16[272,512]{1,0:T(8,128)(2,1)S(1)}, bf16[272,512]{1,0:T(8,128)(2,1)S(1)}, u32[]{:S(2)}, u32[]{:S(2)}) collective-permute-start(bf16[272,512]{1,0:T(8,128)(2,1)S(1)} %collective-permute-done.2), channel_id=1, source_target_pairs={{0,7},{1,0},{2,1},{3,2},{4,3},{5,4},{6,5},{7,6},{8,15},{9,8},{10,9... | collective-permute-start | bytes 835592 | tf_op jit(solution)/shard_map/ppermute | solution.py:116
  95.1 1.9 %collective-permute-start.7 = (bf16[144,512]{1,0:T(8,128)(2,1)S(1)}, bf16[144,512]{1,0:T(8,128)(2,1)S(1)}, u32[]{:S(2)}, u32[]{:S(2)}) collective-permute-start(bf16[144,512]{1,0:T(8,128)(2,1)S(1)} %slice.62), channel_id=1, source_target_pairs={{0,2},{1,3},{2,4},{3,5},{4,6},{5,7},{6,0},{7,1},{8,10},{9,11},{10,... | collective-permute-start | bytes 442376 | tf_op jit(solution)/shard_map/ppermute | solution.py:116
  97.0 5.5 %collective-permute-start.6 = (bf16[128,512]{1,0:T(8,128)(2,1)S(1)}, bf16[128,512]{1,0:T(8,128)(2,1)S(1)}, u32[]{:S(2)}, u32[]{:S(2)}) collective-permute-start(bf16[128,512]{1,0:T(8,128)(2,1)S(1)} %slice.61), channel_id=1, source_target_pairs={{0,6},{1,7},{2,0},{3,1},{4,2},{5,3},{6,4},{7,5},{8,14},{9,15},{10,... | collective-permute-start | bytes 393224 | tf_op jit(solution)/shard_map/ppermute | solution.py:116
  102.5 1.5 %fusion.13 = f32[256,768]{1,0:T(8,128)S(1)} fusion(bf16[4096,768]{1,0:T(8,128)(2,1)} %param.12, s32[]{:T(128)S(6)} %select_n.25, bf16[272,512]{1,0:T(8,128)(2,1)S(1)} %collective-permute-done), kind=kOutput, calls=%fused_computation.18 | convolution fusion | flops 201326592 | bytes 1835012 | tf_op jit(solution)/shard_map/dot_general | solution.py:149
  104.0 1.5 %convolution_add_fusion.4 = f32[256,768]{1,0:T(8,128)S(1)} fusion(f32[256,768]{1,0:T(8,128)S(1)} %fusion.13, bf16[4096,768]{1,0:T(8,128)(2,1)} %param.12, s32[]{:T(128)S(6)} %select_n.24, bf16[272,512]{1,0:T(8,128)(2,1)S(1)} %shard_map.78), kind=kOutput, calls=%fused_computation.8 | convolution fusion | flops 201523200 | bytes 2621444 | tf_op jit(solution)/shard_map/dot_general | solution.py:149
  105.5 0.0 copy-start.8
  105.5 1.6 %convolution_add_fusion.3 = f32[256,768]{1,0:T(8,128)S(1)} fusion(f32[256,768]{1,0:T(8,128)S(1)} %convolution_add_fusion.4, bf16[4096,768]{1,0:T(8,128)(2,1)} %param.12, s32[]{:T(128)S(6)} %select_n.26, bf16[272,512]{1,0:T(8,128)(2,1)S(1)} %collective-permute-done.1), kind=kOutput, calls=%fused_computation.7 | convolution fusion | flops 201523200 | bytes 2621444 | tf_op jit(solution)/shard_map/dot_general | solution.py:149
  107.1 0.0 copy-done.7
  107.1 0.4 convolution_add_fusion.2
  107.5 0.4 convolution_add_fusion.1
  107.9 0.0 collective-permute-done.7
  107.9 0.0 collective-permute-done.6
  107.9 0.4 fusion.5
  108.3 0.0 collective-permute-done.5
  108.3 0.0 collective-permute-done.4
  108.4 0.4 fusion.7
  108.8 0.0 copy-done.8
  108.8 1.2 %fusion.4 = bf16[256,768]{1,0:T(8,128)(2,1)} fusion(f32[256,768]{1,0:T(8,128)S(1)} %fusion.5, f32[256,768]{1,0:T(8,128)S(1)} %fusion.7, f32[256,768]{1,0:T(8,128)S(1)} %convolution_add_fusion.1, bf16[256,768]{1,0:T(8,128)(2,1)S(1)} %copy-done.8, bf16[4096,768]{1,0:T(8,128)(2,1)S(1)} %copy-done.7, s32[]{:T(128)S(6)} %select_n.29, f32[256]{0:T(256)S(1)} %add_rsqrt_fusion, ...), kind=kOutput, calls=%fused_computation.9 | convolution fusion | flops 202702848 | bytes 4195332 | tf_op jit(solution)/shard_map/dot_general | solution.py:149
  (14 shorter events, 0.2 us)
Async XLA Ops:
  0.0 0.9 copy-start
  1.0 0.9 copy-start.2
  28.5 11.1 %all-to-all-start.1 = ((bf16[8,32,128]{2,1,0:T(8,128)(2,1)}), bf16[8,32,128]{2,1,0:T(8,128)(2,1)S(1)}, u32[]{:S(2)}, u32[]{:S(2)}) async-start(bf16[8,32,128]{2,1,0:T(8,128)(2,1)} %shard_map.74), calls=%async_computation.1 | async-start | bytes 131072 | tf_op jit(solution)/shard_map/all_to_all | solution.py:106
  31.9 1.0 copy-start.1
  32.9 0.9 copy-start.3
  33.8 0.9 copy-start.4
  40.3 13.3 %all-to-all-start.2 = ((bf16[16,32,128]{2,1,0:T(8,128)(2,1)}), bf16[16,32,128]{2,1,0:T(8,128)(2,1)S(1)}, u32[]{:S(2)}, u32[]{:S(2)}) async-start(bf16[16,32,128]{2,1,0:T(8,128)(2,1)} %shard_map.76), calls=%async_computation.2 | async-start | bytes 262144 | tf_op jit(solution)/shard_map/all_to_all | solution.py:106
  44.4 0.9 copy-start.5
  45.4 0.7 copy-start.6
  54.0 18.6 %collective-permute-start = (bf16[272,512]{1,0:T(8,128)(2,1)S(1)}, bf16[272,512]{1,0:T(8,128)(2,1)S(1)}, u32[]{:S(2)}, u32[]{:S(2)}) collective-permute-start(bf16[272,512]{1,0:T(8,128)(2,1)S(1)} %shard_map.78), channel_id=1, source_target_pairs={{0,7},{1,0},{2,1},{3,2},{4,3},{5,4},{6,5},{7,6},{8,15},{9,8},{10,9... | collective-permute-start | bytes 835592 | tf_op jit(solution)/shard_map/ppermute | solution.py:116
  66.3 11.7 %collective-permute-start.1 = (bf16[272,512]{1,0:T(8,128)(2,1)S(1)}, bf16[272,512]{1,0:T(8,128)(2,1)S(1)}, u32[]{:S(2)}, u32[]{:S(2)}) collective-permute-start(bf16[272,512]{1,0:T(8,128)(2,1)S(1)} %shard_map.78), channel_id=1, source_target_pairs={{0,1},{1,2},{2,3},{3,4},{4,5},{5,6},{6,7},{7,0},{8,9},{9,10},{10,1... | collective-permute-start | bytes 835592 | tf_op jit(solution)/shard_map/ppermute | solution.py:116
  72.6 10.8 %collective-permute-start.2 = (bf16[272,512]{1,0:T(8,128)(2,1)S(1)}, bf16[272,512]{1,0:T(8,128)(2,1)S(1)}, u32[]{:S(2)}, u32[]{:S(2)}) collective-permute-start(bf16[272,512]{1,0:T(8,128)(2,1)S(1)} %collective-permute-done), channel_id=1, source_target_pairs={{0,7},{1,0},{2,1},{3,2},{4,3},{5,4},{6,5},{7,6},{8,15},{9,8},{10,9... | collective-permute-start | bytes 835592 | tf_op jit(solution)/shard_map/ppermute | solution.py:116
  78.0 10.5 %collective-permute-start.3 = (bf16[272,512]{1,0:T(8,128)(2,1)S(1)}, bf16[272,512]{1,0:T(8,128)(2,1)S(1)}, u32[]{:S(2)}, u32[]{:S(2)}) collective-permute-start(bf16[272,512]{1,0:T(8,128)(2,1)S(1)} %collective-permute-done.1), channel_id=1, source_target_pairs={{0,1},{1,2},{2,3},{3,4},{4,5},{5,6},{6,7},{7,0},{8,9},{9,10},{10,1... | collective-permute-start | bytes 835592 | tf_op jit(solution)/shard_map/ppermute | solution.py:116
  79.9 27.1 %copy-start.7 = (bf16[4096,768]{1,0:T(8,128)(2,1)S(1)}, bf16[4096,768]{1,0:T(8,128)(2,1)}, u32[]{:S(2)}) copy-start(bf16[4096,768]{1,0:T(8,128)(2,1)} %param.12) | copy-start | bytes 18874372
  88.5 19.8 %collective-permute-start.5 = (bf16[272,512]{1,0:T(8,128)(2,1)S(1)}, bf16[272,512]{1,0:T(8,128)(2,1)S(1)}, u32[]{:S(2)}, u32[]{:S(2)}) collective-permute-start(bf16[272,512]{1,0:T(8,128)(2,1)S(1)} %collective-permute-done.3), channel_id=1, source_target_pairs={{0,1},{1,2},{2,3},{3,4},{4,5},{5,6},{6,7},{7,0},{8,9},{9,10},{10,1... | collective-permute-start | bytes 835592 | tf_op jit(solution)/shard_map/ppermute | solution.py:116
  90.5 17.9 %collective-permute-start.4 = (bf16[272,512]{1,0:T(8,128)(2,1)S(1)}, bf16[272,512]{1,0:T(8,128)(2,1)S(1)}, u32[]{:S(2)}, u32[]{:S(2)}) collective-permute-start(bf16[272,512]{1,0:T(8,128)(2,1)S(1)} %collective-permute-done.2), channel_id=1, source_target_pairs={{0,7},{1,0},{2,1},{3,2},{4,3},{5,4},{6,5},{7,6},{8,15},{9,8},{10,9... | collective-permute-start | bytes 835592 | tf_op jit(solution)/shard_map/ppermute | solution.py:116
  95.1 12.8 %collective-permute-start.7 = (bf16[144,512]{1,0:T(8,128)(2,1)S(1)}, bf16[144,512]{1,0:T(8,128)(2,1)S(1)}, u32[]{:S(2)}, u32[]{:S(2)}) collective-permute-start(bf16[144,512]{1,0:T(8,128)(2,1)S(1)} %slice.62), channel_id=1, source_target_pairs={{0,2},{1,3},{2,4},{3,5},{4,6},{5,7},{6,0},{7,1},{8,10},{9,11},{10,... | collective-permute-start | bytes 442376 | tf_op jit(solution)/shard_map/ppermute | solution.py:116
  97.0 10.9 %collective-permute-start.6 = (bf16[128,512]{1,0:T(8,128)(2,1)S(1)}, bf16[128,512]{1,0:T(8,128)(2,1)S(1)}, u32[]{:S(2)}, u32[]{:S(2)}) collective-permute-start(bf16[128,512]{1,0:T(8,128)(2,1)S(1)} %slice.61), channel_id=1, source_target_pairs={{0,6},{1,7},{2,0},{3,1},{4,2},{5,3},{6,4},{7,5},{8,14},{9,15},{10,... | collective-permute-start | bytes 393224 | tf_op jit(solution)/shard_map/ppermute | solution.py:116
  105.5 3.3 %copy-start.8 = (bf16[256,768]{1,0:T(8,128)(2,1)S(1)}, bf16[256,768]{1,0:T(8,128)(2,1)}, u32[]{:S(2)}) copy-start(bf16[256,768]{1,0:T(8,128)(2,1)} %param.13) | copy-start | bytes 1179652

commit v4 on v3

--- a/solution.py
+++ b/solution.py
@@ -112,48 +112,43 @@
     return lax.ppermute(block, ("core", "z"), pairs)
 
 
-def shift(block, hops):
-    return lax.ppermute(block, "z", [(z, (z + hops) % SIDE) for z in range(SIDE)])
-
-
-def gather_seven(block, tokens):
-    one = two = block
-    pieces = [(block, 0)]
-    for step in range(1, SIDE // 2):
-        one, two = ring(one, 1), ring(two, -1)
-        pieces += [(one, step), (two, -step)]
-    pieces.append((ring(one, 1), SIDE // 2))
+def swap(block):
+    return lax.ppermute(block, "core", [(0, 1), (1, 0)])
+
+
+def project(block, weight, residual):
+    tokens = residual.shape[0]
+    width = block.shape[1]
+    z = lax.axis_index("z")
     behind = 2 * lax.axis_index("core") - 1
-    return [(piece, offset * behind) for piece, offset in pieces]
-
-
-def gather_three(block, tokens):
-    half = tokens // 2
-    up1, down1 = shift(block, -1), shift(block, 1)
-    up2, down2 = shift(up1, -1), shift(down1, 1)
-    block, up1, down1, up2, down2 = lax.optimization_barrier((block, up1, down1, up2, down2))
-    up3, down3 = shift(up2, -1), shift(down2, 1)
-    far = jnp.concatenate([shift(up2[:half], -2), shift(down2[half:], 2)], axis=0)
-    return [(block, 0), (up1, 1), (down1, -1), (up2, 2), (down2, -2), (up3, 3), (down3, -3), (far, 4)]
-
-
-def finish(pieces, weight, residual):
-    tokens = residual.shape[0]
-    z = lax.axis_index("z")
-    total = jnp.zeros((tokens,), f32)
-    projected = None
-    for piece, offset in pieces:
-        width = piece.shape[1]
-        source = lax.rem(z + offset + SIDE, SIDE)
+    fence = lax.optimization_barrier
+
+    def product(piece, offset):
+        source = lax.rem(z + offset * behind + SIDE, SIDE)
         rows = lax.dynamic_slice_in_dim(weight, source * width, width, 0)
-        part = jnp.dot(piece[:tokens], rows, preferred_element_type=f32)
-        total = total + jnp.sum(piece[tokens : tokens + 3, :tokens].astype(f32), axis=0)
-        projected = part if projected is None else projected + part
+        return jnp.dot(piece[:tokens], rows, preferred_element_type=f32)
+
+    def squares(piece):
+        return jnp.sum(piece[tokens : tokens + 3, :tokens].astype(f32), axis=0)
+
+    mine1 = ring(block, 1)
+    other1 = ring(swap(block), 1)
+    mine2, other2 = ring(mine1, 1), ring(other1, 1)
+    mine3, other3 = ring(mine2, 1), ring(other2, 1)
+    mine4 = ring(mine3, 1)
+
+    other1, other2, other3 = fence((other1, other2, other3))
+    others = [(other1, 1), (other2, 2), (other3, 3)]
+    partial = sum(product(piece, offset) for piece, offset in others).astype(bf16)
+    partial_squares = sum(squares(piece) for piece, _ in others)
+    block, mine1, mine2, mine3, partial = fence((block, mine1, mine2, mine3, partial))
+    partial, partial_squares = swap(partial), swap(partial_squares)
+
+    own = [(block, 0), (mine1, 1), (mine2, 2), (mine3, 3), (mine4, 4)]
+    projected = sum(product(piece, offset) for piece, offset in own) + partial.astype(f32)
+    total = sum(squares(piece) for piece, _ in own) + partial_squares
     scale_rows = lax.rsqrt(total / INNER + epsilon)
     return (projected * scale_rows[:, None] + residual.astype(f32)).astype(bf16)
-
-
-gather = gather_three
 
 
 def on_device(queries, keys, values, gate_logits, norm_gain, out_weight, residual):
@@ -191,7 +186,7 @@
         attend_kernel, shape((tokens + 16, width), bf16), [VMEM] * 4,
         (queries, state, local, gated), flops=2 * tokens * width * HEAD_DIM,
     )
-    return finish(gather(block, tokens), out_weight, residual)
+    return project(block, out_weight, residual)
 
 
 def solution(mesh):

time: 111 us -> 108 us (0.973)
  waiting for transfers between devices: 24.6 us -> 14.6 us
  starting transfers between devices: 42.7 us -> 50.4 us
    ppermute x8 -> x10, waiting for transfers between devices: 13 us -> 2.9 us  [the longest x7 2.46 us: ring(): return lax.ppermute(block, ('core', 'z'), pairs)]
    ppermute x8 -> x10, starting transfers between devices: 35.3 us -> 43 us  [the longest x7 35.2 us: ring(): return lax.ppermute(block, ('core', 'z'), pairs)]
  transfers between devices with their start and end apart: 10 -> 12, of which waited for: 5 -> 6; matrix products, arithmetic and copies ran while one was open for 5% -> 6% of each run, Pallas kernels for 1% -> 1%
where the time goes in v4:
time: 108 us
  starting transfers between devices  50.4 us (47%)
  blocking collectives  25.7 us (24%)
  waiting for transfers between devices  14.6 us (14%)
  matrix products  7.24 us (7%)
  local copies, waits for them, and re-layouts  6.42 us (6%)
  Pallas kernels  2.75 us (3%)
    ppermute x7, starting transfers between devices, ring(): return lax.ppermute(block, ('core', 'z'), pairs)  35.2 us
    all_to_all x1, blocking collectives, exchange(): return lax.all_to_all(blocks, axes, 0, 0, tiled=True)  25.7 us
    all_to_all x2, waiting for transfers between devices, exchange(): return lax.all_to_all(blocks, axes, 0, 0, tiled=True)  11.7 us
    ppermute x3, starting transfers between devices, swap(): return lax.ppermute(block, 'core', [(0, 1), (1, 0)])  7.82 us
    all_to_all x2, starting transfers between devices, exchange(): return lax.all_to_all(blocks, axes, 0, 0, tiled=True)  7.43 us
    dot_general x8, matrix products, product(): return jnp.dot(piece[:tokens], rows, preferred_element_type=f32)  7.24 us
    unnamed x18, local copies, waits for them, and re-layouts  6.42 us
    pallas_call x6, Pallas kernels, call(): pl.pallas_call(kernel, out_shape=out_shape, in_specs=specs, out_specs=jax...  2.75 us
  transfers between devices with their start and end apart: 12, of which 6 were waited for; matrix products, arithmetic and copies ran while one was open for 6% of the time, Pallas kernels for 1%

profile of v4, /device:TPU:1, one launch (start us, length us, event | category | flops | bytes accessed | tf_op | source)
XLA Modules:
  0.0 107.5 jit_solution(1863376878970036118)
XLA Ops:
  0.0 0.9 copy-done
  1.0 0.9 copy-done.2
  1.9 0.3 shard_map.73
  2.2 25.7 %all_to_all.15.row = bf16[16,32,128]{2,1,0:T(8,128)(2,1)S(1)} all-to-all(bf16[16,32,128]{2,1,0:T(8,128)(2,1)S(1)} %shard_map.73), channel_id=1, replica_groups=mesh['y'=8,'x'=8,'core'=2,'z'=8] {'x','core'}, dimensions={0} | all-to-all | bytes 262144 | tf_op jit(solution)/shard_map/all_to_all | solution.py:106
  27.9 0.7 shard_map.74
  28.5 3.4 %all-to-all-start.1 = ((bf16[8,32,128]{2,1,0:T(8,128)(2,1)}), bf16[8,32,128]{2,1,0:T(8,128)(2,1)S(1)}, u32[]{:S(2)}, u32[]{:S(2)}) async-start(bf16[8,32,128]{2,1,0:T(8,128)(2,1)} %shard_map.74), calls=%async_computation.1 | async-start | bytes 131072 | tf_op jit(solution)/shard_map/all_to_all | solution.py:106
  31.9 0.0 copy-start.1
  31.9 0.9 copy-done.1
  32.9 0.9 copy-done.3
  33.8 0.9 copy-done.4
  34.8 0.7 shard_map.75
  35.4 4.2 %all-to-all-done.1.totals = bf16[8,32,128]{2,1,0:T(8,128)(2,1)S(1)} async-done(((bf16[8,32,128]{2,1,0:T(8,128)(2,1)}), bf16[8,32,128]{2,1,0:T(8,128)(2,1)S(1)}, u32[]{:S(2)}, u32[]{:S(2)}) %all-to-all-start.1) | async-done | bytes 65568 | tf_op jit(solution)/shard_map/all_to_all | solution.py:106
  39.6 0.7 shard_map.76
  40.3 4.1 %all-to-all-start.2 = ((bf16[16,32,128]{2,1,0:T(8,128)(2,1)}), bf16[16,32,128]{2,1,0:T(8,128)(2,1)S(1)}, u32[]{:S(2)}, u32[]{:S(2)}) async-start(bf16[16,32,128]{2,1,0:T(8,128)(2,1)} %shard_map.76), calls=%async_computation.2 | async-start | bytes 262144 | tf_op jit(solution)/shard_map/all_to_all | solution.py:106
  44.4 0.9 copy-done.5
  45.4 0.7 copy-done.6
  46.1 0.1 shard_map.77.gated
  46.2 7.4 %all-to-all-done.2 = bf16[16,32,128]{2,1,0:T(8,128)(2,1)S(1)} async-done(((bf16[16,32,128]{2,1,0:T(8,128)(2,1)}), bf16[16,32,128]{2,1,0:T(8,128)(2,1)S(1)}, u32[]{:S(2)}, u32[]{:S(2)}) %all-to-all-start.2) | async-done | bytes 131104 | tf_op jit(solution)/shard_map/all_to_all | solution.py:106
  53.6 0.4 shard_map.78
  54.0 1.9 %collective-permute-start.3 = (bf16[272,512]{1,0:T(8,128)(2,1)S(1)}, bf16[272,512]{1,0:T(8,128)(2,1)S(1)}, u32[]{:S(2)}, u32[]{:S(2)}) collective-permute-start(bf16[272,512]{1,0:T(8,128)(2,1)S(1)} %shard_map.78), channel_id=1, source_target_pairs={{0,8},{8,0},{1,9},{9,1},{2,10},{10,2},{3,11},{11,3},{4,12},{12,4},... | collective-permute-start | bytes 835592 | tf_op jit(solution)/shard_map/ppermute | solution.py:116
  55.9 12.3 %collective-permute-start = (bf16[272,512]{1,0:T(8,128)(2,1)S(1)}, bf16[272,512]{1,0:T(8,128)(2,1)S(1)}, u32[]{:S(2)}, u32[]{:S(2)}) collective-permute-start(bf16[272,512]{1,0:T(8,128)(2,1)S(1)} %shard_map.78), channel_id=1, source_target_pairs={{0,1},{1,2},{2,3},{3,4},{4,5},{5,6},{6,7},{7,0},{8,15},{9,8},{10,9... | collective-permute-start | bytes 835592 | tf_op jit(solution)/shard_map/ppermute | solution.py:112
  68.2 0.0 collective-permute-done.3
  68.2 1.9 %collective-permute-start.4 = (bf16[272,512]{1,0:T(8,128)(2,1)S(1)}, bf16[272,512]{1,0:T(8,128)(2,1)S(1)}, u32[]{:S(2)}, u32[]{:S(2)}) collective-permute-start(bf16[272,512]{1,0:T(8,128)(2,1)S(1)} %collective-permute-done.3), channel_id=1, source_target_pairs={{0,1},{1,2},{2,3},{3,4},{4,5},{5,6},{6,7},{7,0},{8,15},{9,8},{10,9... | collective-permute-start | bytes 835592 | tf_op jit(solution)/shard_map/ppermute | solution.py:112
  70.2 1.5 %collective-permute-done = bf16[272,512]{1,0:T(8,128)(2,1)S(1)} collective-permute-done((bf16[272,512]{1,0:T(8,128)(2,1)S(1)}, bf16[272,512]{1,0:T(8,128)(2,1)S(1)}, u32[]{:S(2)}, u32[]{:S(2)}) %collective-permute-start) | collective-permute-done | bytes 278560 | tf_op jit(solution)/shard_map/ppermute | solution.py:112
  71.7 5.0 %collective-permute-start.1 = (bf16[272,512]{1,0:T(8,128)(2,1)S(1)}, bf16[272,512]{1,0:T(8,128)(2,1)S(1)}, u32[]{:S(2)}, u32[]{:S(2)}) collective-permute-start(bf16[272,512]{1,0:T(8,128)(2,1)S(1)} %collective-permute-done), channel_id=1, source_target_pairs={{0,1},{1,2},{2,3},{3,4},{4,5},{5,6},{6,7},{7,0},{8,15},{9,8},{10,9... | collective-permute-start | bytes 835592 | tf_op jit(solution)/shard_map/ppermute | solution.py:112
  76.7 0.0 collective-permute-done.4
  76.7 3.0 %collective-permute-start.5 = (bf16[272,512]{1,0:T(8,128)(2,1)S(1)}, bf16[272,512]{1,0:T(8,128)(2,1)S(1)}, u32[]{:S(2)}, u32[]{:S(2)}) collective-permute-start(bf16[272,512]{1,0:T(8,128)(2,1)S(1)} %collective-permute-done.4), channel_id=1, source_target_pairs={{0,1},{1,2},{2,3},{3,4},{4,5},{5,6},{6,7},{7,0},{8,15},{9,8},{10,9... | collective-permute-start | bytes 835592 | tf_op jit(solution)/shard_map/ppermute | solution.py:112
  79.7 0.5 collective-permute-done.1
  80.2 5.0 %collective-permute-start.2 = (bf16[272,512]{1,0:T(8,128)(2,1)S(1)}, bf16[272,512]{1,0:T(8,128)(2,1)S(1)}, u32[]{:S(2)}, u32[]{:S(2)}) collective-permute-start(bf16[272,512]{1,0:T(8,128)(2,1)S(1)} %collective-permute-done.1), channel_id=1, source_target_pairs={{0,1},{1,2},{2,3},{3,4},{4,5},{5,6},{6,7},{7,0},{8,15},{9,8},{10,9... | collective-permute-start | bytes 835592 | tf_op jit(solution)/shard_map/ppermute | solution.py:112
  85.2 0.0 collective-permute-done.5
  85.2 3.0 %collective-permute-start.6 = (bf16[272,512]{1,0:T(8,128)(2,1)S(1)}, bf16[272,512]{1,0:T(8,128)(2,1)S(1)}, u32[]{:S(2)}, u32[]{:S(2)}) collective-permute-start(bf16[272,512]{1,0:T(8,128)(2,1)S(1)} %collective-permute-done.5), channel_id=1, source_target_pairs={{0,1},{1,2},{2,3},{3,4},{4,5},{5,6},{6,7},{7,0},{8,15},{9,8},{10,9... | collective-permute-start | bytes 835592 | tf_op jit(solution)/shard_map/ppermute | solution.py:112
  88.2 0.0 copy-start.7
  88.3 0.4 collective-permute-done.2
  88.7 5.0 %collective-permute-start.7 = (bf16[272,512]{1,0:T(8,128)(2,1)S(1)}, bf16[272,512]{1,0:T(8,128)(2,1)S(1)}, u32[]{:S(2)}, u32[]{:S(2)}) collective-permute-start(bf16[272,512]{1,0:T(8,128)(2,1)S(1)} %collective-permute-done.2), channel_id=1, source_target_pairs={{0,1},{1,2},{2,3},{3,4},{4,5},{5,6},{6,7},{7,0},{8,15},{9,8},{10,9... | collective-permute-start | bytes 835592 | tf_op jit(solution)/shard_map/ppermute | solution.py:112
  93.7 0.0 collective-permute-done.6
  93.8 1.5 %fusion.10 = f32[256,768]{1,0:T(8,128)S(1)} fusion(bf16[4096,768]{1,0:T(8,128)(2,1)} %param.12, s32[]{:T(128)S(6)} %select_n.19, bf16[272,512]{1,0:T(8,128)(2,1)S(1)} %collective-permute-done.5), kind=kOutput, calls=%fused_computation.16 | convolution fusion | flops 201326592 | bytes 1835012 | tf_op jit(solution)/shard_map/dot_general | solution.py:129
  95.3 1.5 %convolution_add_fusion.5 = f32[256,768]{1,0:T(8,128)S(1)} fusion(f32[256,768]{1,0:T(8,128)S(1)} %fusion.10, bf16[4096,768]{1,0:T(8,128)(2,1)} %param.12, s32[]{:T(128)S(6)} %select_n.18, bf16[272,512]{1,0:T(8,128)(2,1)S(1)} %collective-permute-done.4), kind=kOutput, calls=%fused_computation.8 | convolution fusion | flops 201523200 | bytes 2621444 | tf_op jit(solution)/shard_map/dot_general | solution.py:129
  96.8 0.0 copy-start.8
  96.8 1.6 %fusion.3 = bf16[256,768]{1,0:T(8,128)(2,1)S(1)} fusion(f32[256,768]{1,0:T(8,128)S(1)} %convolution_add_fusion.5, bf16[4096,768]{1,0:T(8,128)(2,1)} %param.12, s32[]{:T(128)S(6)} %select_n.20, bf16[272,512]{1,0:T(8,128)(2,1)S(1)} %collective-permute-done.6), kind=kOutput, calls=%fused_computation.9 | convolution fusion | flops 201719808 | bytes 2228228 | tf_op jit(solution)/shard_map/dot_general | solution.py:129
  98.4 4.0 %collective-permute-start.9 = (f32[256]{0:T(256)S(1)}, f32[256]{0:T(256)S(1)}, u32[]{:S(2)}, u32[]{:S(2)}) collective-permute-start(f32[256]{0:T(256)S(1)} %add_add_fusion), channel_id=1, source_target_pairs={{0,8},{8,0},{1,9},{9,1},{2,10},{10,2},{3,11},{11,3},{4,12},{12,4},... | collective-permute-start | bytes 3080 | tf_op jit(solution)/shard_map/ppermute | solution.py:116
  102.4 0.4 fusion.12
  102.7 1.9 %collective-permute-start.8 = (bf16[256,768]{1,0:T(8,128)(2,1)S(1)}, bf16[256,768]{1,0:T(8,128)(2,1)S(1)}, u32[]{:S(2)}, u32[]{:S(2)}) collective-permute-start(bf16[256,768]{1,0:T(8,128)(2,1)S(1)} %fusion.3), channel_id=1, source_target_pairs={{0,8},{8,0},{1,9},{9,1},{2,10},{10,2},{3,11},{11,3},{4,12},{12,4},... | collective-permute-start | bytes 1179656 | tf_op jit(solution)/shard_map/ppermute | solution.py:116
  104.7 0.4 convolution_add_fusion.3
  105.1 0.4 convolution_add_fusion.2
  105.4 0.4 convolution_add_fusion.1
  105.9 0.0 collective-permute-done.7
  105.9 0.4 collective-permute-done.8
  106.4 1.2 %fusion.4 = bf16[256,768]{1,0:T(8,128)(2,1)} fusion(f32[256,768]{1,0:T(8,128)S(1)} %convolution_add_fusion.1, bf16[256,768]{1,0:T(8,128)(2,1)S(1)} %copy-done.8, bf16[256,768]{1,0:T(8,128)(2,1)S(1)} %collective-permute-done.8, bf16[4096,768]{1,0:T(8,128)(2,1)S(1)} %copy-done.7, s32[]{:T(128)S(6)} %select_n.22, f32[256]{0:T(256)S(1)} %add_rsqrt_fusion, ...), kind=kOutput, calls=%fused_computation.10 | convolution fusion | flops 202702848 | bytes 3015684 | tf_op jit(solution)/shard_map/dot_general | solution.py:129
  (16 shorter events, 0.1 us)
Async XLA Ops:
  0.0 0.9 copy-start
  1.0 0.9 copy-start.2
  28.5 11.1 %all-to-all-start.1 = ((bf16[8,32,128]{2,1,0:T(8,128)(2,1)}), bf16[8,32,128]{2,1,0:T(8,128)(2,1)S(1)}, u32[]{:S(2)}, u32[]{:S(2)}) async-start(bf16[8,32,128]{2,1,0:T(8,128)(2,1)} %shard_map.74), calls=%async_computation.1 | async-start | bytes 131072 | tf_op jit(solution)/shard_map/all_to_all | solution.py:106
  31.9 1.0 copy-start.1
  32.9 0.9 copy-start.3
  33.8 0.9 copy-start.4
  40.3 13.3 %all-to-all-start.2 = ((bf16[16,32,128]{2,1,0:T(8,128)(2,1)}), bf16[16,32,128]{2,1,0:T(8,128)(2,1)S(1)}, u32[]{:S(2)}, u32[]{:S(2)}) async-start(bf16[16,32,128]{2,1,0:T(8,128)(2,1)} %shard_map.76), calls=%async_computation.2 | async-start | bytes 262144 | tf_op jit(solution)/shard_map/all_to_all | solution.py:106
  44.4 0.9 copy-start.5
  45.4 0.7 copy-start.6
  54.0 14.2 %collective-permute-start.3 = (bf16[272,512]{1,0:T(8,128)(2,1)S(1)}, bf16[272,512]{1,0:T(8,128)(2,1)S(1)}, u32[]{:S(2)}, u32[]{:S(2)}) collective-permute-start(bf16[272,512]{1,0:T(8,128)(2,1)S(1)} %shard_map.78), channel_id=1, source_target_pairs={{0,8},{8,0},{1,9},{9,1},{2,10},{10,2},{3,11},{11,3},{4,12},{12,4},... | collective-permute-start | bytes 835592 | tf_op jit(solution)/shard_map/ppermute | solution.py:116
  55.9 15.8 %collective-permute-start = (bf16[272,512]{1,0:T(8,128)(2,1)S(1)}, bf16[272,512]{1,0:T(8,128)(2,1)S(1)}, u32[]{:S(2)}, u32[]{:S(2)}) collective-permute-start(bf16[272,512]{1,0:T(8,128)(2,1)S(1)} %shard_map.78), channel_id=1, source_target_pairs={{0,1},{1,2},{2,3},{3,4},{4,5},{5,6},{6,7},{7,0},{8,15},{9,8},{10,9... | collective-permute-start | bytes 835592 | tf_op jit(solution)/shard_map/ppermute | solution.py:112
  68.2 8.5 %collective-permute-start.4 = (bf16[272,512]{1,0:T(8,128)(2,1)S(1)}, bf16[272,512]{1,0:T(8,128)(2,1)S(1)}, u32[]{:S(2)}, u32[]{:S(2)}) collective-permute-start(bf16[272,512]{1,0:T(8,128)(2,1)S(1)} %collective-permute-done.3), channel_id=1, source_target_pairs={{0,1},{1,2},{2,3},{3,4},{4,5},{5,6},{6,7},{7,0},{8,15},{9,8},{10,9... | collective-permute-start | bytes 835592 | tf_op jit(solution)/shard_map/ppermute | solution.py:112
  71.7 8.5 %collective-permute-start.1 = (bf16[272,512]{1,0:T(8,128)(2,1)S(1)}, bf16[272,512]{1,0:T(8,128)(2,1)S(1)}, u32[]{:S(2)}, u32[]{:S(2)}) collective-permute-start(bf16[272,512]{1,0:T(8,128)(2,1)S(1)} %collective-permute-done), channel_id=1, source_target_pairs={{0,1},{1,2},{2,3},{3,4},{4,5},{5,6},{6,7},{7,0},{8,15},{9,8},{10,9... | collective-permute-start | bytes 835592 | tf_op jit(solution)/shard_map/ppermute | solution.py:112
  76.7 8.5 %collective-permute-start.5 = (bf16[272,512]{1,0:T(8,128)(2,1)S(1)}, bf16[272,512]{1,0:T(8,128)(2,1)S(1)}, u32[]{:S(2)}, u32[]{:S(2)}) collective-permute-start(bf16[272,512]{1,0:T(8,128)(2,1)S(1)} %collective-permute-done.4), channel_id=1, source_target_pairs={{0,1},{1,2},{2,3},{3,4},{4,5},{5,6},{6,7},{7,0},{8,15},{9,8},{10,9... | collective-permute-start | bytes 835592 | tf_op jit(solution)/shard_map/ppermute | solution.py:112
  80.2 8.5 %collective-permute-start.2 = (bf16[272,512]{1,0:T(8,128)(2,1)S(1)}, bf16[272,512]{1,0:T(8,128)(2,1)S(1)}, u32[]{:S(2)}, u32[]{:S(2)}) collective-permute-start(bf16[272,512]{1,0:T(8,128)(2,1)S(1)} %collective-permute-done.1), channel_id=1, source_target_pairs={{0,1},{1,2},{2,3},{3,4},{4,5},{5,6},{6,7},{7,0},{8,15},{9,8},{10,9... | collective-permute-start | bytes 835592 | tf_op jit(solution)/shard_map/ppermute | solution.py:112
  85.2 8.5 %collective-permute-start.6 = (bf16[272,512]{1,0:T(8,128)(2,1)S(1)}, bf16[272,512]{1,0:T(8,128)(2,1)S(1)}, u32[]{:S(2)}, u32[]{:S(2)}) collective-permute-start(bf16[272,512]{1,0:T(8,128)(2,1)S(1)} %collective-permute-done.5), channel_id=1, source_target_pairs={{0,1},{1,2},{2,3},{3,4},{4,5},{5,6},{6,7},{7,0},{8,15},{9,8},{10,9... | collective-permute-start | bytes 835592 | tf_op jit(solution)/shard_map/ppermute | solution.py:112
  88.2 14.1 %copy-start.7 = (bf16[4096,768]{1,0:T(8,128)(2,1)S(1)}, bf16[4096,768]{1,0:T(8,128)(2,1)}, u32[]{:S(2)}) copy-start(bf16[4096,768]{1,0:T(8,128)(2,1)} %param.12) | copy-start | bytes 18874372
  88.7 17.2 %collective-permute-start.7 = (bf16[272,512]{1,0:T(8,128)(2,1)S(1)}, bf16[272,512]{1,0:T(8,128)(2,1)S(1)}, u32[]{:S(2)}, u32[]{:S(2)}) collective-permute-start(bf16[272,512]{1,0:T(8,128)(2,1)S(1)} %collective-permute-done.2), channel_id=1, source_target_pairs={{0,1},{1,2},{2,3},{3,4},{4,5},{5,6},{6,7},{7,0},{8,15},{9,8},{10,9... | collective-permute-start | bytes 835592 | tf_op jit(solution)/shard_map/ppermute | solution.py:112
  96.8 9.6 %copy-start.8 = (bf16[256,768]{1,0:T(8,128)(2,1)S(1)}, bf16[256,768]{1,0:T(8,128)(2,1)}, u32[]{:S(2)}) copy-start(bf16[256,768]{1,0:T(8,128)(2,1)} %param.13) | copy-start | bytes 1179652
  98.4 7.5 %collective-permute-start.9 = (f32[256]{0:T(256)S(1)}, f32[256]{0:T(256)S(1)}, u32[]{:S(2)}, u32[]{:S(2)}) collective-permute-start(f32[256]{0:T(256)S(1)} %add_add_fusion), channel_id=1, source_target_pairs={{0,8},{8,0},{1,9},{9,1},{2,10},{10,2},{3,11},{11,3},{4,12},{12,4},... | collective-permute-start | bytes 3080 | tf_op jit(solution)/shard_map/ppermute | solution.py:116
  102.7 3.6 %collective-permute-start.8 = (bf16[256,768]{1,0:T(8,128)(2,1)S(1)}, bf16[256,768]{1,0:T(8,128)(2,1)S(1)}, u32[]{:S(2)}, u32[]{:S(2)}) collective-permute-start(bf16[256,768]{1,0:T(8,128)(2,1)S(1)} %fusion.3), channel_id=1, source_target_pairs={{0,8},{8,0},{1,9},{9,1},{2,10},{10,2},{3,11},{11,3},{4,12},{12,4},... | collective-permute-start | bytes 1179656 | tf_op jit(solution)/shard_map/ppermute | solution.py:116

commit v5 on v4

--- a/solution.py
+++ b/solution.py
@@ -6,11 +6,13 @@
 from jax.sharding import Mesh, PartitionSpec as P
 
 HEAD_DIM = 128
-BLOCK = 256
 INNER = 4096
 SIDE = 8
 CORES = 2
+EXTRA = 16
 LIMIT = 12 * 2**20
+MOST = 48 * 2**20
+ALL = (60 * 1024 - 192) * 2**10
 
 epsilon = 1e-06
 f32 = jnp.float32
@@ -21,14 +23,18 @@
 SMEM = pl.BlockSpec(memory_space=pltpu.SMEM)
 
 
-def call(kernel, out_shape, specs, args, flops=0):
+ANY = pl.BlockSpec(memory_space=pl.ANY)
+
+
+def call(kernel, out_shape, specs, args, scratch=(), flops=0, limit=LIMIT):
     size = sum(a.size * a.dtype.itemsize for a in args)
     return pl.pallas_call(
         kernel,
         out_shape=out_shape,
         in_specs=specs,
         out_specs=jax.tree.map(lambda _: VMEM, out_shape),
-        compiler_params=pltpu.CompilerParams(vmem_limit_bytes=LIMIT),
+        scratch_shapes=scratch,
+        compiler_params=pltpu.CompilerParams(vmem_limit_bytes=limit),
         cost_estimate=pl.CostEstimate(flops=flops, bytes_accessed=size, transcendentals=0),
     )(*args)
 
@@ -37,7 +43,15 @@
     return [slice(h * HEAD_DIM, (h + 1) * HEAD_DIM) for h in range(ref.shape[1] // HEAD_DIM)]
 
 
-def state_kernel(keys, values, out):
+def state_kernel(keys_hbm, values_hbm, out, keys, values, semaphores):
+    copies = [
+        pltpu.make_async_copy(keys_hbm, keys, semaphores.at[0]),
+        pltpu.make_async_copy(values_hbm, values, semaphores.at[1]),
+    ]
+    for copy in copies:
+        copy.start()
+    for copy in copies:
+        copy.wait()
     rows = out.shape[1]
     per = HEAD_DIM // rows
     for h, cols in enumerate(heads_of(keys)):
@@ -102,6 +116,54 @@
     out[tokens:, tokens:] = jnp.zeros((extra, out.shape[1] - tokens), bf16)
 
 
+def fetch(places, weight, buffers, semaphores):
+    copies = []
+    for n, buffer in enumerate(buffers):
+        width = buffer.shape[0]
+        rows = weight.at[pl.ds(places[n] * width, width), :]
+        copies.append(pltpu.make_async_copy(rows, buffer, semaphores.at[n]))
+        copies[-1].start()
+    return copies
+
+
+def accumulate(pieces, copies, buffers, tokens):
+    total = None
+    squares = jnp.zeros((1, tokens), f32)
+    for piece, copy, buffer in zip(pieces, copies, buffers):
+        extra = piece[tokens:, :tokens].astype(f32)
+        squares = squares + jnp.sum(extra[:3], axis=0, keepdims=True)
+        copy.wait()
+        part = jnp.dot(piece[:tokens], buffer[...], preferred_element_type=f32)
+        total = part if total is None else total + part
+    return total, squares
+
+
+def other_kernel(places, one, two, three, weight, out, rows, semaphores):
+    tokens = one.shape[0] - EXTRA
+    buffers = [rows.at[n] for n in range(3)]
+    copies = fetch(places, weight, buffers, semaphores)
+    total, squares = accumulate([one, two, three], copies, buffers, tokens)
+    out[:tokens] = total.astype(bf16)
+    high = squares.astype(bf16).astype(f32)
+    middle = (squares - high).astype(bf16).astype(f32)
+    low = squares - high - middle
+    extra = out.shape[0] - tokens
+    place = lax.broadcasted_iota(jnp.int32, (extra, tokens), 0)
+    packed = jnp.where(place == 0, high, jnp.where(place == 1, middle, jnp.where(place == 2, low, 0.0)))
+    out[tokens:, :tokens] = packed.astype(bf16)
+    out[tokens:, tokens:] = jnp.zeros((extra, out.shape[1] - tokens), bf16)
+
+
+def own_kernel(places, block, one, two, three, weight, out, squares_out, last, rows, semaphores):
+    tokens = out.shape[0]
+    buffers = [rows.at[n] for n in range(4)]
+    copies = fetch(places, weight, buffers + [last], semaphores)
+    total, squares = accumulate([block, one, two, three], copies[:4], buffers, tokens)
+    out[...] = total
+    squares_out[...] = jnp.broadcast_to(squares, squares_out.shape)
+    copies[4].wait()
+
+
 def exchange(blocks, axes):
     return lax.all_to_all(blocks, axes, 0, 0, tiled=True)
 
@@ -117,19 +179,18 @@
 
 
 def project(block, weight, residual):
-    tokens = residual.shape[0]
+    tokens, columns = residual.shape
     width = block.shape[1]
     z = lax.axis_index("z")
     behind = 2 * lax.axis_index("core") - 1
     fence = lax.optimization_barrier
-
-    def product(piece, offset):
-        source = lax.rem(z + offset * behind + SIDE, SIDE)
-        rows = lax.dynamic_slice_in_dim(weight, source * width, width, 0)
-        return jnp.dot(piece[:tokens], rows, preferred_element_type=f32)
-
-    def squares(piece):
-        return jnp.sum(piece[tokens : tokens + 3, :tokens].astype(f32), axis=0)
+    shape = jax.ShapeDtypeStruct
+
+    def source(offset):
+        return lax.rem(z + offset * behind + SIDE, SIDE)
+
+    def places(offsets):
+        return jnp.stack([source(offset) for offset in offsets])
 
     mine1 = ring(block, 1)
     other1 = ring(swap(block), 1)
@@ -137,16 +198,29 @@
     mine3, other3 = ring(mine2, 1), ring(other2, 1)
     mine4 = ring(mine3, 1)
 
-    other1, other2, other3 = fence((other1, other2, other3))
-    others = [(other1, 1), (other2, 2), (other3, 3)]
-    partial = sum(product(piece, offset) for piece, offset in others).astype(bf16)
-    partial_squares = sum(squares(piece) for piece, _ in others)
+    partial = call(
+        other_kernel, shape((block.shape[0], columns), bf16), [SMEM] + [VMEM] * 3 + [ANY],
+        (places([1, 2, 3]), other1, other2, other3, weight),
+        [pltpu.VMEM((3, width, columns), bf16), pltpu.SemaphoreType.DMA((3,))],
+        flops=6 * tokens * width * columns, limit=MOST,
+    )
     block, mine1, mine2, mine3, partial = fence((block, mine1, mine2, mine3, partial))
-    partial, partial_squares = swap(partial), swap(partial_squares)
-
-    own = [(block, 0), (mine1, 1), (mine2, 2), (mine3, 3), (mine4, 4)]
-    projected = sum(product(piece, offset) for piece, offset in own) + partial.astype(f32)
-    total = sum(squares(piece) for piece, _ in own) + partial_squares
+    partial = swap(partial)
+    projected, squares, last = call(
+        own_kernel,
+        [shape((tokens, columns), f32), shape((8, tokens), f32), shape((width, columns), bf16)],
+        [SMEM] + [VMEM] * 4 + [ANY],
+        (places([0, 1, 2, 3, 4]), block, mine1, mine2, mine3, weight),
+        [pltpu.VMEM((4, width, columns), bf16), pltpu.SemaphoreType.DMA((5,))],
+        flops=8 * tokens * width * columns, limit=MOST,
+    )
+
+    def squares_of(piece):
+        return jnp.sum(piece[tokens : tokens + 3, :tokens].astype(f32), axis=0)
+
+    projected = projected + jnp.dot(mine4[:tokens], last, preferred_element_type=f32)
+    projected = projected + partial[:tokens].astype(f32)
+    total = squares[0] + squares_of(partial) + squares_of(mine4)
     scale_rows = lax.rsqrt(total / INNER + epsilon)
     return (projected * scale_rows[:, None] + residual.astype(f32)).astype(bf16)
 
@@ -162,28 +236,30 @@
     chunk = shape((row_places, rows, HEAD_DIM), bf16)
 
     own = call(
-        state_kernel, chunk, [VMEM] * 2, (keys, values), flops=2 * tokens * width * HEAD_DIM
+        state_kernel, chunk, [ANY] * 2, (keys, values),
+        [pltpu.VMEM((tokens, width), bf16)] * 2 + [pltpu.SemaphoreType.DMA((2,))],
+        flops=2 * tokens * width * HEAD_DIM, limit=ALL,
     )
     row = exchange(own, ("x", "core"))
     totals = call(total_kernel, shape((SIDE, rows, HEAD_DIM), bf16), [VMEM], (row,))
-    totals, queries = lax.optimization_barrier((totals, queries))
+    totals, gate_logits = lax.optimization_barrier((totals, gate_logits))
     totals = exchange(totals, "y")
-    local, queries = call(
-        local_kernel, [wide, tile], [VMEM] * 3, (queries, keys, values),
-        flops=4 * tokens * tokens * width,
-    )
-    y_place = lax.axis_index("y").reshape(1)
-    totals, local = lax.optimization_barrier((totals, local))
-    state = call(prefix_kernel, chunk, [SMEM, VMEM, VMEM], (y_place, row, totals))
-    state, gate_logits = lax.optimization_barrier((state, gate_logits))
-    state = exchange(state, ("x", "core")).reshape(heads, HEAD_DIM, HEAD_DIM)
     z_place = lax.axis_index("z").reshape(1)
     gated = call(
         gate_kernel, wide, [SMEM, VMEM, VMEM],
         (z_place, norm_gain.reshape(-1, HEAD_DIM), gate_logits), flops=tokens * width,
     )
+    totals, gated = lax.optimization_barrier((totals, gated))
+    y_place = lax.axis_index("y").reshape(1)
+    state = call(prefix_kernel, chunk, [SMEM, VMEM, VMEM], (y_place, row, totals))
+    state, queries = lax.optimization_barrier((state, queries))
+    state = exchange(state, ("x", "core")).reshape(heads, HEAD_DIM, HEAD_DIM)
+    local, queries = call(
+        local_kernel, [wide, tile], [VMEM] * 3, (queries, keys, values),
+        flops=4 * tokens * tokens * width,
+    )
     block = call(
-        attend_kernel, shape((tokens + 16, width), bf16), [VMEM] * 4,
+        attend_kernel, shape((tokens + EXTRA, width), bf16), [VMEM] * 4,
         (queries, state, local, gated), flops=2 * tokens * width * HEAD_DIM,
     )
     return project(block, out_weight, residual)

time: 108 us -> 108 us (level)
  Pallas kernels: 2.75 us -> 10.6 us
  matrix products: 7.24 us -> 1.17 us
  starting transfers between devices: 50.4 us -> 45.9 us
  waiting for transfers between devices: 14.6 us -> 18.4 us
  local copies, waits for them, and re-layouts: 6.42 us -> 4.6 us
    pallas_call x6 -> x8, Pallas kernels: 2.75 us -> 10.6 us  [call(): pl.pallas_call(kernel, out_shape=out_shape, in_specs=specs, out_specs=jax...]
    dot_general x8 -> x1, matrix products: 7.24 us -> 1.17 us  [project(): jnp.dot(mine4[:tokens], last, preferred_element_type=f32)]
    ppermute x7, starting transfers between devices: 35.2 us -> 32.1 us  [ring(): return lax.ppermute(block, ('core', 'z'), pairs)]
    ppermute x7, waiting for transfers between devices: 2.46 us -> 5.23 us  [ring(): return lax.ppermute(block, ('core', 'z'), pairs)]
    unnamed x18 -> x12, local copies, waits for them, and re-layouts: 6.42 us -> 4.51 us
    ppermute x3 -> x2, starting transfers between devices: 7.82 us -> 6.43 us  [swap(): return lax.ppermute(block, 'core', [(0, 1), (1, 0)])]
    ppermute x3 -> x2, waiting for transfers between devices: 0.44 us -> 1.53 us  [swap(): return lax.ppermute(block, 'core', [(0, 1), (1, 0)])]
  transfers between devices with their start and end apart: 12 -> 11, of which waited for: 6 -> 8; matrix products, arithmetic and copies ran while one was open for 6% -> 0% of each run, Pallas kernels for 1% -> 6%
where the time goes in v5:
time: 108 us
  starting transfers between devices  45.9 us (42%)
  blocking collectives  26.6 us (25%)
  waiting for transfers between devices  18.4 us (17%)
  Pallas kernels  10.6 us (10%)
  local copies, waits for them, and re-layouts  4.6 us (4%)
  matrix products  1.17 us (1%)
    ppermute x7, starting transfers between devices, ring(): return lax.ppermute(block, ('core', 'z'), pairs)  32.1 us
    all_to_all x1, blocking collectives, exchange(): return lax.all_to_all(blocks, axes, 0, 0, tiled=True)  26.6 us
    all_to_all x2, waiting for transfers between devices, exchange(): return lax.all_to_all(blocks, axes, 0, 0, tiled=True)  11.7 us
    pallas_call x8, Pallas kernels, call(): pl.pallas_call(kernel, out_shape=out_shape, in_specs=specs, out_specs=jax...  10.6 us
    all_to_all x2, starting transfers between devices, exchange(): return lax.all_to_all(blocks, axes, 0, 0, tiled=True)  7.43 us
    ppermute x2, starting transfers between devices, swap(): return lax.ppermute(block, 'core', [(0, 1), (1, 0)])  6.43 us
    ppermute x7, waiting for transfers between devices, ring(): return lax.ppermute(block, ('core', 'z'), pairs)  5.23 us
    unnamed x12, local copies, waits for them, and re-layouts  4.51 us
  transfers between devices with their start and end apart: 11, of which 8 were waited for; matrix products, arithmetic and copies ran while one was open for 0% of the time, Pallas kernels for 6%

profile of v5, /device:TPU:1, one launch (start us, length us, event | category | flops | bytes accessed | tf_op | source)
XLA Modules:
  0.0 107.7 jit_solution(13724616537933047491)
XLA Ops:
  0.0 2.0 %shard_map.73 = bf16[16,32,128]{2,1,0:T(8,128)(2,1)} custom-call(bf16[256,512]{1,0:T(8,128)(2,1)} %keys.1, bf16[256,512]{1,0:T(8,128)(2,1)} %values.1), custom_call_target="tpu_custom_call" | custom-call | flops 33554432 | bytes 524288 | tf_op jit(solution)/shard_map/pallas_call | solution.py:31
  2.0 26.6 %all_to_all.15.row = bf16[16,32,128]{2,1,0:T(8,128)(2,1)S(1)} all-to-all(bf16[16,32,128]{2,1,0:T(8,128)(2,1)} %shard_map.73), channel_id=1, replica_groups=mesh['y'=8,'x'=8,'core'=2,'z'=8] {'x','core'}, dimensions={0} | all-to-all | bytes 262144 | tf_op jit(solution)/shard_map/all_to_all | solution.py:168
  28.6 0.7 shard_map.74
  29.2 3.4 %all-to-all-start.1 = ((bf16[8,32,128]{2,1,0:T(8,128)(2,1)}), bf16[8,32,128]{2,1,0:T(8,128)(2,1)S(1)}, u32[]{:S(2)}, u32[]{:S(2)}) async-start(bf16[8,32,128]{2,1,0:T(8,128)(2,1)} %shard_map.74), calls=%async_computation.1 | async-start | bytes 131072 | tf_op jit(solution)/shard_map/all_to_all | solution.py:168
  32.6 0.0 copy-start.3
  32.6 0.9 copy-done.3
  33.5 0.0 copy-start.4
  33.5 0.7 copy-done.4
  34.3 0.1 shard_map.75.gated
  34.3 6.0 %all-to-all-done.1.totals = bf16[8,32,128]{2,1,0:T(8,128)(2,1)S(1)} async-done(((bf16[8,32,128]{2,1,0:T(8,128)(2,1)}), bf16[8,32,128]{2,1,0:T(8,128)(2,1)S(1)}, u32[]{:S(2)}, u32[]{:S(2)}) %all-to-all-start.1) | async-done | bytes 65568 | tf_op jit(solution)/shard_map/all_to_all | solution.py:168
  40.3 0.7 shard_map.76
  41.0 4.1 %all-to-all-start.2 = ((bf16[16,32,128]{2,1,0:T(8,128)(2,1)}), bf16[16,32,128]{2,1,0:T(8,128)(2,1)S(1)}, u32[]{:S(2)}, u32[]{:S(2)}) async-start(bf16[16,32,128]{2,1,0:T(8,128)(2,1)} %shard_map.76), calls=%async_computation.2 | async-start | bytes 262144 | tf_op jit(solution)/shard_map/all_to_all | solution.py:168
  45.1 0.0 copy-start
  45.1 0.9 copy-done
  46.1 0.0 copy-start.1
  46.1 0.9 copy-done.1
  47.0 0.0 copy-start.2
  47.0 0.9 copy-done.2
  48.0 0.7 shard_map.77
  48.6 5.7 %all-to-all-done.2 = bf16[16,32,128]{2,1,0:T(8,128)(2,1)S(1)} async-done(((bf16[16,32,128]{2,1,0:T(8,128)(2,1)}), bf16[16,32,128]{2,1,0:T(8,128)(2,1)S(1)}, u32[]{:S(2)}, u32[]{:S(2)}) %all-to-all-start.2) | async-done | bytes 131104 | tf_op jit(solution)/shard_map/all_to_all | solution.py:168
  54.3 0.4 shard_map.78.block
  54.7 1.9 %collective-permute-start.3 = (bf16[272,512]{1,0:T(8,128)(2,1)S(1)}, bf16[272,512]{1,0:T(8,128)(2,1)S(1)}, u32[]{:S(2)}, u32[]{:S(2)}) collective-permute-start(bf16[272,512]{1,0:T(8,128)(2,1)S(1)} %shard_map.78.block), channel_id=1, source_target_pairs={{0,8},{8,0},{1,9},{9,1},{2,10},{10,2},{3,11},{11,3},{4,12},{12,4},... | collective-permute-start | bytes 835592 | tf_op jit(solution)/shard_map/ppermute | solution.py:178
  56.6 1.5 %collective-permute-done.3 = bf16[272,512]{1,0:T(8,128)(2,1)S(1)} collective-permute-done((bf16[272,512]{1,0:T(8,128)(2,1)S(1)}, bf16[272,512]{1,0:T(8,128)(2,1)S(1)}, u32[]{:S(2)}, u32[]{:S(2)}) %collective-permute-start.3) | collective-permute-done | bytes 278560 | tf_op jit(solution)/shard_map/ppermute | solution.py:178
  58.2 11.6 %collective-permute-start.4 = (bf16[272,512]{1,0:T(8,128)(2,1)S(1)}, bf16[272,512]{1,0:T(8,128)(2,1)S(1)}, u32[]{:S(2)}, u32[]{:S(2)}) collective-permute-start(bf16[272,512]{1,0:T(8,128)(2,1)S(1)} %collective-permute-done.3), channel_id=1, source_target_pairs={{0,1},{1,2},{2,3},{3,4},{4,5},{5,6},{6,7},{7,0},{8,15},{9,8},{10,9... | collective-permute-start | bytes 835592 | tf_op jit(solution)/shard_map/ppermute | solution.py:174
  69.8 1.9 %collective-permute-start = (bf16[272,512]{1,0:T(8,128)(2,1)S(1)}, bf16[272,512]{1,0:T(8,128)(2,1)S(1)}, u32[]{:S(2)}, u32[]{:S(2)}) collective-permute-start(bf16[272,512]{1,0:T(8,128)(2,1)S(1)} %shard_map.78.block), channel_id=1, source_target_pairs={{0,1},{1,2},{2,3},{3,4},{4,5},{5,6},{6,7},{7,0},{8,15},{9,8},{10,9... | collective-permute-start | bytes 835592 | tf_op jit(solution)/shard_map/ppermute | solution.py:174
  71.7 1.5 %collective-permute-done.4.one = bf16[272,512]{1,0:T(8,128)(2,1)S(1)} collective-permute-done((bf16[272,512]{1,0:T(8,128)(2,1)S(1)}, bf16[272,512]{1,0:T(8,128)(2,1)S(1)}, u32[]{:S(2)}, u32[]{:S(2)}) %collective-permute-start.4) | collective-permute-done | bytes 278560 | tf_op jit(solution)/shard_map/ppermute | solution.py:174
  73.2 5.0 %collective-permute-start.5 = (bf16[272,512]{1,0:T(8,128)(2,1)S(1)}, bf16[272,512]{1,0:T(8,128)(2,1)S(1)}, u32[]{:S(2)}, u32[]{:S(2)}) collective-permute-start(bf16[272,512]{1,0:T(8,128)(2,1)S(1)} %collective-permute-done.4.one), channel_id=1, source_target_pairs={{0,1},{1,2},{2,3},{3,4},{4,5},{5,6},{6,7},{7,0},{8,15},{9,8},{10,9... | collective-permute-start | bytes 835592 | tf_op jit(solution)/shard_map/ppermute | solution.py:174
  78.2 0.0 collective-permute-done.one
  78.3 3.0 %collective-permute-start.1 = (bf16[272,512]{1,0:T(8,128)(2,1)S(1)}, bf16[272,512]{1,0:T(8,128)(2,1)S(1)}, u32[]{:S(2)}, u32[]{:S(2)}) collective-permute-start(bf16[272,512]{1,0:T(8,128)(2,1)S(1)} %collective-permute-done.one), channel_id=1, source_target_pairs={{0,1},{1,2},{2,3},{3,4},{4,5},{5,6},{6,7},{7,0},{8,15},{9,8},{10,9... | collective-permute-start | bytes 835592 | tf_op jit(solution)/shard_map/ppermute | solution.py:174
  81.2 0.5 collective-permute-done.5.two
  81.7 5.0 %collective-permute-start.6 = (bf16[272,512]{1,0:T(8,128)(2,1)S(1)}, bf16[272,512]{1,0:T(8,128)(2,1)S(1)}, u32[]{:S(2)}, u32[]{:S(2)}) collective-permute-start(bf16[272,512]{1,0:T(8,128)(2,1)S(1)} %collective-permute-done.5.two), channel_id=1, source_target_pairs={{0,1},{1,2},{2,3},{3,4},{4,5},{5,6},{6,7},{7,0},{8,15},{9,8},{10,9... | collective-permute-start | bytes 835592 | tf_op jit(solution)/shard_map/ppermute | solution.py:174
  86.7 0.0 collective-permute-done.1.two
  86.8 3.0 %collective-permute-start.2 = (bf16[272,512]{1,0:T(8,128)(2,1)S(1)}, bf16[272,512]{1,0:T(8,128)(2,1)S(1)}, u32[]{:S(2)}, u32[]{:S(2)}) collective-permute-start(bf16[272,512]{1,0:T(8,128)(2,1)S(1)} %collective-permute-done.1.two), channel_id=1, source_target_pairs={{0,1},{1,2},{2,3},{3,4},{4,5},{5,6},{6,7},{7,0},{8,15},{9,8},{10,9... | collective-permute-start | bytes 835592 | tf_op jit(solution)/shard_map/ppermute | solution.py:174
  89.7 0.1 pad_add_fusion.places
  89.8 0.0 copy-start.5
  89.8 0.4 collective-permute-done.6.three
  90.2 2.9 %shard_map.79 = bf16[272,768]{1,0:T(8,128)(2,1)S(1)} custom-call(s32[3]{0:T(128)S(1)} %pad_add_fusion.places, bf16[272,512]{1,0:T(8,128)(2,1)S(1)} %collective-permute-done.4.one, bf16[272,512]{1,0:T(8,128)(2,1)S(1)} %collective-permute-done.5.two, bf16[272,512]{1,0:T(8,128)(2,1)S(1)} %collective-permute-done.6.three, bf16[4096,768]{1,0:T(8,128)(2,1)} %weight.3), custom_call_target="tpu_custom_call" | custom-call | flops 603979776 | bytes 7127052 | tf_op jit(solution)/shard_map/pallas_call | solution.py:31
  93.1 1.2 %collective-permute-done.2.three = bf16[272,512]{1,0:T(8,128)(2,1)S(1)} collective-permute-done((bf16[272,512]{1,0:T(8,128)(2,1)S(1)}, bf16[272,512]{1,0:T(8,128)(2,1)S(1)}, u32[]{:S(2)}, u32[]{:S(2)}) %collective-permute-start.2) | collective-permute-done | bytes 278560 | tf_op jit(solution)/shard_map/ppermute | solution.py:174
  94.3 4.5 %collective-permute-start.8 = (bf16[272,768]{1,0:T(8,128)(2,1)S(1)}, bf16[272,768]{1,0:T(8,128)(2,1)S(1)}, u32[]{:S(2)}, u32[]{:S(2)}) collective-permute-start(bf16[272,768]{1,0:T(8,128)(2,1)S(1)} %shard_map.79), channel_id=1, source_target_pairs={{0,8},{8,0},{1,9},{9,1},{2,10},{10,2},{3,11},{11,3},{4,12},{12,4},... | collective-permute-start | bytes 1253384 | tf_op jit(solution)/shard_map/ppermute | solution.py:178
  98.9 2.6 %collective-permute-start.7 = (bf16[272,512]{1,0:T(8,128)(2,1)S(1)}, bf16[272,512]{1,0:T(8,128)(2,1)S(1)}, u32[]{:S(2)}, u32[]{:S(2)}) collective-permute-start(bf16[272,512]{1,0:T(8,128)(2,1)S(1)} %collective-permute-done.2.three), channel_id=1, source_target_pairs={{0,1},{1,2},{2,3},{3,4},{4,5},{5,6},{6,7},{7,0},{8,15},{9,8},{10,9... | collective-permute-start | bytes 835592 | tf_op jit(solution)/shard_map/ppermute | solution.py:174
  101.5 0.1 stack.29.places
  101.6 3.3 %shard_map.80 = (f32[256,768]{1,0:T(8,128)S(1)}, f32[8,256]{1,0:T(8,128)S(1)}, bf16[512,768]{1,0:T(8,128)(2,1)S(1)}) custom-call(s32[5]{0:T(128)S(1)} %stack.29.places, bf16[272,512]{1,0:T(8,128)(2,1)S(1)} %shard_map.78.block, bf16[272,512]{1,0:T(8,128)(2,1)S(1)} %collective-permute-done.one, bf16[272,512]{1,0:T(8,128)(2,1)S(1)} %collective-permute-done.1.two, ...), custom_call_target="tpu_custom_call" | custom-call | flops 805306368 | bytes 7405588 | tf_op jit(solution)/shard_map/pallas_call | solution.py:31
  104.9 1.6 %collective-permute-done.7 = bf16[272,512]{1,0:T(8,128)(2,1)S(1)} collective-permute-done((bf16[272,512]{1,0:T(8,128)(2,1)S(1)}, bf16[272,512]{1,0:T(8,128)(2,1)S(1)}, u32[]{:S(2)}, u32[]{:S(2)}) %collective-permute-start.7) | collective-permute-done | bytes 278560 | tf_op jit(solution)/shard_map/ppermute | solution.py:174
  106.5 0.0 collective-permute-done.8
  106.5 0.0 copy-done.5
  106.5 1.2 %fusion.3 = bf16[256,768]{1,0:T(8,128)(2,1)} fusion(f32[256,768]{1,0:T(8,128)S(1)} %get-tuple-element.33, bf16[512,768]{1,0:T(8,128)(2,1)S(1)} %get-tuple-element.34, bf16[256,768]{1,0:T(8,128)(2,1)S(1)} %copy-done.5, bf16[272,768]{1,0:T(8,128)(2,1)S(1)} %collective-permute-done.8, f32[256]{0:T(256)S(1)} %add_rsqrt_fusion, ...), kind=kOutput, calls=%fused_computation.4 | convolution fusion | flops 202702848 | bytes 3015680 | tf_op jit(solution)/shard_map/dot_general | solution.py:221
  (4 shorter events, 0.1 us)
Async XLA Ops:
  29.2 11.1 %all-to-all-start.1 = ((bf16[8,32,128]{2,1,0:T(8,128)(2,1)}), bf16[8,32,128]{2,1,0:T(8,128)(2,1)S(1)}, u32[]{:S(2)}, u32[]{:S(2)}) async-start(bf16[8,32,128]{2,1,0:T(8,128)(2,1)} %shard_map.74), calls=%async_computation.1 | async-start | bytes 131072 | tf_op jit(solution)/shard_map/all_to_all | solution.py:168
  32.6 1.0 copy-start.3
  33.5 0.7 copy-start.4
  41.0 13.3 %all-to-all-start.2 = ((bf16[16,32,128]{2,1,0:T(8,128)(2,1)}), bf16[16,32,128]{2,1,0:T(8,128)(2,1)S(1)}, u32[]{:S(2)}, u32[]{:S(2)}) async-start(bf16[16,32,128]{2,1,0:T(8,128)(2,1)} %shard_map.76), calls=%async_computation.2 | async-start | bytes 262144 | tf_op jit(solution)/shard_map/all_to_all | solution.py:168
  45.1 0.9 copy-start
  46.1 0.9 copy-start.1
  47.0 0.9 copy-start.2
  54.7 3.5 %collective-permute-start.3 = (bf16[272,512]{1,0:T(8,128)(2,1)S(1)}, bf16[272,512]{1,0:T(8,128)(2,1)S(1)}, u32[]{:S(2)}, u32[]{:S(2)}) collective-permute-start(bf16[272,512]{1,0:T(8,128)(2,1)S(1)} %shard_map.78.block), channel_id=1, source_target_pairs={{0,8},{8,0},{1,9},{9,1},{2,10},{10,2},{3,11},{11,3},{4,12},{12,4},... | collective-permute-start | bytes 835592 | tf_op jit(solution)/shard_map/ppermute | solution.py:178
  58.2 15.1 %collective-permute-start.4 = (bf16[272,512]{1,0:T(8,128)(2,1)S(1)}, bf16[272,512]{1,0:T(8,128)(2,1)S(1)}, u32[]{:S(2)}, u32[]{:S(2)}) collective-permute-start(bf16[272,512]{1,0:T(8,128)(2,1)S(1)} %collective-permute-done.3), channel_id=1, source_target_pairs={{0,1},{1,2},{2,3},{3,4},{4,5},{5,6},{6,7},{7,0},{8,15},{9,8},{10,9... | collective-permute-start | bytes 835592 | tf_op jit(solution)/shard_map/ppermute | solution.py:174
  69.8 8.5 %collective-permute-start = (bf16[272,512]{1,0:T(8,128)(2,1)S(1)}, bf16[272,512]{1,0:T(8,128)(2,1)S(1)}, u32[]{:S(2)}, u32[]{:S(2)}) collective-permute-start(bf16[272,512]{1,0:T(8,128)(2,1)S(1)} %shard_map.78.block), channel_id=1, source_target_pairs={{0,1},{1,2},{2,3},{3,4},{4,5},{5,6},{6,7},{7,0},{8,15},{9,8},{10,9... | collective-permute-start | bytes 835592 | tf_op jit(solution)/shard_map/ppermute | solution.py:174
  73.2 8.5 %collective-permute-start.5 = (bf16[272,512]{1,0:T(8,128)(2,1)S(1)}, bf16[272,512]{1,0:T(8,128)(2,1)S(1)}, u32[]{:S(2)}, u32[]{:S(2)}) collective-permute-start(bf16[272,512]{1,0:T(8,128)(2,1)S(1)} %collective-permute-done.4.one), channel_id=1, source_target_pairs={{0,1},{1,2},{2,3},{3,4},{4,5},{5,6},{6,7},{7,0},{8,15},{9,8},{10,9... | collective-permute-start | bytes 835592 | tf_op jit(solution)/shard_map/ppermute | solution.py:174
  78.3 8.5 %collective-permute-start.1 = (bf16[272,512]{1,0:T(8,128)(2,1)S(1)}, bf16[272,512]{1,0:T(8,128)(2,1)S(1)}, u32[]{:S(2)}, u32[]{:S(2)}) collective-permute-start(bf16[272,512]{1,0:T(8,128)(2,1)S(1)} %collective-permute-done.one), channel_id=1, source_target_pairs={{0,1},{1,2},{2,3},{3,4},{4,5},{5,6},{6,7},{7,0},{8,15},{9,8},{10,9... | collective-permute-start | bytes 835592 | tf_op jit(solution)/shard_map/ppermute | solution.py:174
  81.7 8.5 %collective-permute-start.6 = (bf16[272,512]{1,0:T(8,128)(2,1)S(1)}, bf16[272,512]{1,0:T(8,128)(2,1)S(1)}, u32[]{:S(2)}, u32[]{:S(2)}) collective-permute-start(bf16[272,512]{1,0:T(8,128)(2,1)S(1)} %collective-permute-done.5.two), channel_id=1, source_target_pairs={{0,1},{1,2},{2,3},{3,4},{4,5},{5,6},{6,7},{7,0},{8,15},{9,8},{10,9... | collective-permute-start | bytes 835592 | tf_op jit(solution)/shard_map/ppermute | solution.py:174
  86.8 7.6 %collective-permute-start.2 = (bf16[272,512]{1,0:T(8,128)(2,1)S(1)}, bf16[272,512]{1,0:T(8,128)(2,1)S(1)}, u32[]{:S(2)}, u32[]{:S(2)}) collective-permute-start(bf16[272,512]{1,0:T(8,128)(2,1)S(1)} %collective-permute-done.1.two), channel_id=1, source_target_pairs={{0,1},{1,2},{2,3},{3,4},{4,5},{5,6},{6,7},{7,0},{8,15},{9,8},{10,9... | collective-permute-start | bytes 835592 | tf_op jit(solution)/shard_map/ppermute | solution.py:174
  89.8 16.7 %copy-start.5 = (bf16[256,768]{1,0:T(8,128)(2,1)S(1)}, bf16[256,768]{1,0:T(8,128)(2,1)}, u32[]{:S(2)}) copy-start(bf16[256,768]{1,0:T(8,128)(2,1)} %param.13) | copy-start | bytes 1179652
  94.3 12.1 %collective-permute-start.8 = (bf16[272,768]{1,0:T(8,128)(2,1)S(1)}, bf16[272,768]{1,0:T(8,128)(2,1)S(1)}, u32[]{:S(2)}, u32[]{:S(2)}) collective-permute-start(bf16[272,768]{1,0:T(8,128)(2,1)S(1)} %shard_map.79), channel_id=1, source_target_pairs={{0,8},{8,0},{1,9},{9,1},{2,10},{10,2},{3,11},{11,3},{4,12},{12,4},... | collective-permute-start | bytes 1253384 | tf_op jit(solution)/shard_map/ppermute | solution.py:178
  98.9 7.6 %collective-permute-start.7 = (bf16[272,512]{1,0:T(8,128)(2,1)S(1)}, bf16[272,512]{1,0:T(8,128)(2,1)S(1)}, u32[]{:S(2)}, u32[]{:S(2)}) collective-permute-start(bf16[272,512]{1,0:T(8,128)(2,1)S(1)} %collective-permute-done.2.three), channel_id=1, source_target_pairs={{0,1},{1,2},{2,3},{3,4},{4,5},{5,6},{6,7},{7,0},{8,15},{9,8},{10,9... | collective-permute-start | bytes 835592 | tf_op jit(solution)/shard_map/ppermute | solution.py:174
